TPU v7x, 128 devices: a whole 4x4x4 slice. The times are simulated.
128 devices in a mesh: harm: 8 (over x_hi, y), gx: 4 (over z), gz: 4 (over x_lo, core).
Axes of the slice: x: 4 (x_hi: 2, x_lo: 2; x = x_hi * 2 + x_lo), y: 4, z: 4, core: 2. Of those that a mesh axis runs over, the one named last changes fastest.
Arguments:
- perturbation: bfloat16 [32, 2, 4, 128, 24, 128], P('harm', None, None, 'gx', 'gz'), may hold values from -6 to 6
- base_mean: bfloat16 [3, 128, 24, 128], P(None, 'gx', 'gz'), may hold values from -6 to 6
- base_modes: bfloat16 [2, 2, 3, 128, 24, 128], P(None, None, None, 'gx', 'gz'), may hold values from -3 to 3
- solid_mask: int32 [128, 24, 128], P('gx', 'gz'), may hold values from 0 to 1, as said below
Outputs:
- residual_harmonics: float32 [32, 2, 4, 128, 24, 128], P('harm', None, None, 'gx', 'gz')
Inputs may be any that keep to these rules, and one draw needn't show every extreme that they name: `solid_mask`: 1 on the cells of one circular cylinder of radius 2 or more cells in the x-y plane, the same at every spanwise position, 0 elsewhere.
All inputs are finite; a program needn't handle non-finite values.
Results may differ from a plain program's by a relative error of at most 0.0003.
Values may be sent and summed in bfloat16 or wider, within the bound.
A program may use at most 128 MiB of HBM per device.

v0:
```python
import jax
import jax.numpy as jnp
from jax import lax
from jax.experimental import pallas as pl
from jax.experimental.pallas import tpu as pltpu
from jax.sharding import PartitionSpec as P

FREQUENCY_STEP = 0.2
VISCOSITY = 0.05
PENALTY = 4.0
EDGE = 8
ROWS = 48


def with_halo(shard, sides, width, wrap):
    for axis, dim in sides:
        size, length = (lax.axis_size(axis), shard.shape[dim])
        up = [(i, (i + 1) % size) for i in range(size if wrap else size - 1)]
        down = [(j, i) for i, j in up]
        last = lax.slice_in_dim(shard, length - width, length, axis=dim)
        first = lax.slice_in_dim(shard, 0, width, axis=dim)
        before = lax.ppermute(last, axis, up)
        after = lax.ppermute(first, axis, down)
        shard = jnp.concatenate([before, shard, after], axis=dim)
    return shard


def vel(l, part, c):
    return (l * 2 + part) * 3 + c


def pres(l, part):
    return 48 + l * 2 + part


def base(m, part, c):
    return 56 + c if m == 0 else 59 + ((m - 1) * 2 + part) * 3 + c


def block(slabs, mask_ref, out_ref, masks, freqs, z, xb):
    row = xb * 8 + EDGE

    def load(field, dz=0, dx=0):
        return slabs[field, z + 2 + dz, pl.ds(row + dx, 8), :]

    def lane(value, offset):
        return jnp.where(masks[offset], pltpu.roll(value, (-offset) % 128, 1), 0.0)

    def sides(field, d):
        if d == 0:
            return tuple(load(field, 0, o) for o in (1, -1, 2, -2))
        if d == 2:
            return tuple(load(field, o, 0) for o in (1, -1, 2, -2))
        value = load(field)
        return tuple(lane(value, o) for o in (1, -1, 2, -2))

    def slope(s):
        return 8.0 * (s[0] - s[1]) - (s[2] - s[3])

    solid = PENALTY * mask_ref[z, pl.ds(xb * 8, 8), :].astype(jnp.float32)
    flow = {
        (m, part, d): load(base(m, part, d)) * (1.0 / 12.0)
        for m in range(3)
        for part in range(1 if m == 0 else 2)
        for d in range(3)
    }
    diverge = {}
    for c in range(3):
        bend = {
            (m, part, d): slope(sides(base(m, part, c), d)) * (1.0 / 12.0)
            for m in range(3)
            for part in range(1 if m == 0 else 2)
            for d in range(3)
        }
        total = {}
        for l in range(8):
            own = 2 <= l < 6
            grad = {}
            for part in range(2):
                around = [sides(vel(l, part, c), d) for d in range(3)]
                for d in range(3):
                    grad[part, d] = slope(around[d])
                if own:
                    value = load(vel(l, part, c))
                    near = sum(s[0] + s[1] for s in around)
                    far = sum(s[2] + s[3] for s in around)
                    other = load(vel(l, 1 - part, c))
                    turn = freqs[l - 2] * other
                    start = (
                        solid * value
                        - (VISCOSITY * 16.0 / 12.0) * near
                        + (VISCOSITY / 12.0) * far
                        + (VISCOSITY * 90.0 / 12.0) * value
                    )
                    start = start - turn if part == 0 else start + turn
                    k = l - 2
                    start = start + slope(sides(pres(k, part), c)) * (1.0 / 12.0)
                    total[k, part] = start + total[k, part] if (k, part) in total else start
                    key = (k, part)
                    diverge[key] = grad[part, c] + diverge[key] if key in diverge else grad[part, c]
            speed = {(part, d): load(vel(l, part, d)) for part in range(2) for d in range(3)}
            for k in range(4):
                m = k - (l - 2)
                if abs(m) > 2:
                    continue
                a = abs(m)
                pieces_r, pieces_i = [], []
                for d in range(3):
                    gr, gi = grad[0, d], grad[1, d]
                    ur, ui = speed[0, d], speed[1, d]
                    fr, br = flow[a, 0, d], bend[a, 0, d]
                    pieces_r += [fr * gr, ur * br]
                    pieces_i += [fr * gi, ui * br]
                    if a:
                        fi, bi = flow[a, 1, d], bend[a, 1, d]
                        sign = 1 if m > 0 else -1
                        pieces_r += [(-sign, fi * gi), (-sign, ui * bi)]
                        pieces_i += [(sign, fi * gr), (sign, ur * bi)]
                for part, pieces in ((0, pieces_r), (1, pieces_i)):
                    value = total.get((k, part))
                    for piece in pieces:
                        sign, term = piece if isinstance(piece, tuple) else (1, piece)
                        if value is None:
                            value = term if sign > 0 else -term
                        else:
                            value = value + term if sign > 0 else value - term
                    total[k, part] = value
        for k in range(4):
            for part in range(2):
                out_ref[k, part, c, z, pl.ds(xb * 8, 8), :] = total[k, part]
    for k in range(4):
        for part in range(2):
            out_ref[k, part, 3, z, pl.ds(xb * 8, 8), :] = diverge[k, part] * (1.0 / 12.0)


def kernel(vel_ref, pres_ref, base_ref, mask_ref, out_ref, slabs):
    harm = lax.axis_index("harm")
    freqs = [FREQUENCY_STEP * (harm * 4 + k - 16).astype(jnp.float32) for k in range(4)]

    def stage(ref, count, first):
        def body(i, carry):
            slabs[first + i] = ref[i].astype(jnp.float32)
            return carry

        lax.fori_loop(0, count, body, 0)

    stage(vel_ref, 48, 0)
    stage(pres_ref, 8, 48)
    stage(base_ref, 15, 56)
    lanes = lax.broadcasted_iota(jnp.int32, (8, 128), 1)
    masks = {1: lanes < 127, 2: lanes < 126, -1: lanes >= 1, -2: lanes >= 2}

    def layer(z, carry):
        def chunk(xb, inner):
            block(slabs, mask_ref, out_ref, masks, freqs, z, xb)
            return inner

        return lax.fori_loop(0, 4, chunk, carry)

    lax.fori_loop(0, 6, layer, 0)


def shards(perturbation, base_mean, base_modes, solid_mask):
    turned = jnp.transpose(perturbation, (0, 1, 2, 4, 3, 5))
    mean = jnp.transpose(base_mean, (0, 2, 1, 3))
    modes = jnp.transpose(base_modes, (0, 1, 2, 4, 3, 5))
    mask = jnp.transpose(solid_mask, (1, 0, 2))
    per, _, _, cz, cx, cy = turned.shape
    base_all = jnp.concatenate([mean, modes.reshape(12, cz, cx, cy)], 0)
    velocity = with_halo(turned[:, :, :3], (("harm", 0),), 2, False)
    pressure = turned[:, :, 3].reshape(per * 2, cz, cx, cy)
    velocity = velocity.reshape(48, cz, cx, cy)

    def pad(values):
        values = with_halo(values, (("gx", 2), ("gz", 1)), 2, True)
        return jnp.pad(values, ((0, 0), (0, 0), (6, 6), (0, 0)))

    vmem = pl.BlockSpec(memory_space=pltpu.VMEM)
    out = pl.pallas_call(
        kernel,
        out_shape=jax.ShapeDtypeStruct((per, 2, 4, cz, cx, cy), jnp.float32),
        in_specs=[vmem] * 4,
        out_specs=vmem,
        scratch_shapes=[pltpu.VMEM((71, 10, ROWS, 128), jnp.float32)],
        compiler_params=pltpu.CompilerParams(vmem_limit_bytes=60 * 1024 * 1024),
    )(pad(velocity), pad(pressure), pad(base_all), mask)
    return jnp.transpose(out, (0, 1, 2, 4, 3, 5))


def solution(mesh):
    return jax.shard_map(
        shards,
        mesh=mesh,
        in_specs=(
            P("harm", None, None, "gx", "gz", None),
            P(None, "gx", "gz", None),
            P(None, None, None, "gx", "gz", None),
            P("gx", "gz", None),
        ),
        out_specs=P("harm", None, None, "gx", "gz", None),
        check_vma=False,
    )
```

profile of v0, /device:TPU:25, one launch (start us, length us, event | category | flops | bytes accessed | tf_op | source)
XLA Modules:
  0.0 98.5 jit_solution(15097130040259059855)
XLA Ops:
  0.0 1.6 %fusion.21 = (bf16[2,2,3,6,32,128]{5,4,3,2,1,0:T(8,128)(2,1)S(1)}, bf16[2,2,3,6,32,128]{5,4,3,2,1,0:T(8,128)(2,1)S(1)}) fusion(bf16[4,2,4,6,32,128]{5,4,3,2,1,0:T(8,128)(2,1)} %bitcast.15), kind=kLoop, calls=%fused_computation.46 | loop fusion | bytes 2359296 | tf_op jit(solution)/shard_map/slice | solution.py:20
  1.6 4.3 %collective-permute-start = (bf16[2,2,3,6,32,128]{5,4,3,2,1,0:T(8,128)(2,1)S(1)}, bf16[2,2,3,6,32,128]{5,4,3,2,1,0:T(8,128)(2,1)S(1)}, u32[]{:S(2)}, u32[]{:S(2)}) collective-permute-start(bf16[2,2,3,6,32,128]{5,4,3,2,1,0:T(8,128)(2,1)S(1)} %get-tuple-element.9), channel_id=1, source_target_pairs={{0,16},{16,32},{32,48},{48,64},{64,80},{80,96},{96,112},{1,17},{17... | collective-permute-start | bytes 1769480 | tf_op jit(solution)/shard_map/ppermute | solution.py:22
  5.9 1.9 %collective-permute-start.1 = (bf16[2,2,3,6,32,128]{5,4,3,2,1,0:T(8,128)(2,1)S(1)}, bf16[2,2,3,6,32,128]{5,4,3,2,1,0:T(8,128)(2,1)S(1)}, u32[]{:S(2)}, u32[]{:S(2)}) collective-permute-start(bf16[2,2,3,6,32,128]{5,4,3,2,1,0:T(8,128)(2,1)S(1)} %get-tuple-element.10), channel_id=1, source_target_pairs={{16,0},{32,16},{48,32},{64,48},{80,64},{96,80},{112,96},{17,1},{33... | collective-permute-start | bytes 1769480 | tf_op jit(solution)/shard_map/ppermute | solution.py:23
  7.8 0.0 copy-done.1
  7.9 1.7 %collective-permute-start.6 = (bf16[8,6,2,128]{3,2,1,0:T(2,128)(2,1)S(1)}, bf16[8,6,2,128]{3,2,1,0:T(2,128)(2,1)S(1)}, u32[]{:S(2)}, u32[]{:S(2)}) collective-permute-start(bf16[8,6,2,128]{3,2,1,0:T(2,128)(2,1)S(1)} %get-tuple-element.17), channel_id=1, source_target_pairs={{0,4},{4,8},{8,12},{12,0},{1,5},{5,9},{9,13},{13,1},{2,6},{6,10},{... | collective-permute-start | bytes 73736 | tf_op jit(solution)/shard_map/ppermute | solution.py:22
  9.6 2.2 %collective-permute-start.7 = (bf16[8,6,2,128]{3,2,1,0:T(2,128)(2,1)S(1)}, bf16[8,6,2,128]{3,2,1,0:T(2,128)(2,1)S(1)}, u32[]{:S(2)}, u32[]{:S(2)}) collective-permute-start(bf16[8,6,2,128]{3,2,1,0:T(2,128)(2,1)S(1)} %get-tuple-element.18), channel_id=1, source_target_pairs={{4,0},{8,4},{12,8},{0,12},{5,1},{9,5},{13,9},{1,13},{6,2},{10,6},{... | collective-permute-start | bytes 73736 | tf_op jit(solution)/shard_map/ppermute | solution.py:23
  11.8 0.2 slice.67
  12.0 0.0 copy-start
  12.0 0.0 copy-start.2
  12.1 5.8 %collective-permute-done = bf16[2,2,3,6,32,128]{5,4,3,2,1,0:T(8,128)(2,1)S(1)} collective-permute-done((bf16[2,2,3,6,32,128]{5,4,3,2,1,0:T(8,128)(2,1)S(1)}, bf16[2,2,3,6,32,128]{5,4,3,2,1,0:T(8,128)(2,1)S(1)}, u32[]{:S(2)}, u32[]{:S(2)}) %collective-permute-start) | collective-permute-done | bytes 589856 | tf_op jit(solution)/shard_map/ppermute | solution.py:22
  17.9 7.5 %collective-permute-done.1 = bf16[2,2,3,6,32,128]{5,4,3,2,1,0:T(8,128)(2,1)S(1)} collective-permute-done((bf16[2,2,3,6,32,128]{5,4,3,2,1,0:T(8,128)(2,1)S(1)}, bf16[2,2,3,6,32,128]{5,4,3,2,1,0:T(8,128)(2,1)S(1)}, u32[]{:S(2)}, u32[]{:S(2)}) %collective-permute-start.1) | collective-permute-done | bytes 589856 | tf_op jit(solution)/shard_map/ppermute | solution.py:23
  25.3 0.3 pad_maximum_fusion
  25.6 0.2 fusion.20
  25.8 1.7 %collective-permute-start.2 = (bf16[48,6,2,128]{3,2,1,0:T(2,128)(2,1)S(1)}, bf16[48,6,2,128]{3,2,1,0:T(2,128)(2,1)S(1)}, u32[]{:S(2)}, u32[]{:S(2)}) collective-permute-start(bf16[48,6,2,128]{3,2,1,0:T(2,128)(2,1)S(1)} %get-tuple-element.7), channel_id=1, source_target_pairs={{0,4},{4,8},{8,12},{12,0},{1,5},{5,9},{9,13},{13,1},{2,6},{6,10},{... | collective-permute-start | bytes 442376 | tf_op jit(solution)/shard_map/ppermute | solution.py:22
  27.6 2.2 %collective-permute-start.3 = (bf16[48,6,2,128]{3,2,1,0:T(2,128)(2,1)S(1)}, bf16[48,6,2,128]{3,2,1,0:T(2,128)(2,1)S(1)}, u32[]{:S(2)}, u32[]{:S(2)}) collective-permute-start(bf16[48,6,2,128]{3,2,1,0:T(2,128)(2,1)S(1)} %get-tuple-element.8), channel_id=1, source_target_pairs={{4,0},{8,4},{12,8},{0,12},{5,1},{9,5},{13,9},{1,13},{6,2},{10,6},{... | collective-permute-start | bytes 442376 | tf_op jit(solution)/shard_map/ppermute | solution.py:23
  29.8 0.0 copy-done
  29.8 0.1 pad_maximum_fusion.12
  29.8 0.1 collective-permute-start.10
  29.9 0.0 collective-permute-done.6
  29.9 2.7 %collective-permute-start.11 = (bf16[15,6,2,128]{3,2,1,0:T(2,128)(2,1)S(1)}, bf16[15,6,2,128]{3,2,1,0:T(2,128)(2,1)S(1)}, u32[]{:S(2)}, u32[]{:S(2)}) collective-permute-start(bf16[15,6,2,128]{3,2,1,0:T(2,128)(2,1)S(1)} %get-tuple-element.14), channel_id=1, source_target_pairs={{4,0},{8,4},{12,8},{0,12},{5,1},{9,5},{13,9},{1,13},{6,2},{10,6},{... | collective-permute-start | bytes 138248 | tf_op jit(solution)/shard_map/ppermute | solution.py:23
  32.6 0.0 collective-permute-done.7
  32.6 0.2 pad_maximum_fusion.10
  32.7 2.9 %collective-permute-start.8 = (bf16[8,2,36,128]{3,2,1,0:T(8,128)(2,1)S(1)}, bf16[8,2,36,128]{3,2,1,0:T(8,128)(2,1)S(1)}, u32[]{:S(2)}, u32[]{:S(2)}) collective-permute-start(bf16[8,2,36,128]{3,2,1,0:T(8,128)(2,1)S(1)} %get-tuple-element.15), channel_id=1, source_target_pairs={{0,1},{1,2},{2,3},{3,0},{4,5},{5,6},{6,7},{7,4},{8,9},{9,10},{10,1... | collective-permute-start | bytes 442376 | tf_op jit(solution)/shard_map/ppermute | solution.py:22
  35.7 0.0 collective-permute-done.2
  35.7 0.0 collective-permute-start.9
  35.7 0.0 collective-permute-done.3
  35.7 1.3 %pad_maximum_fusion.3 = (bf16[48,2,36,128]{3,2,1,0:T(8,128)(2,1)S(1)}, bf16[48,2,36,128]{3,2,1,0:T(8,128)(2,1)S(1)}) fusion(bf16[48,6,2,128]{3,2,1,0:T(2,128)(2,1)S(1)} %collective-permute-done.3, bf16[48,6,32,128]{3,2,1,0:T(8,128)(2,1)S(1)} %bitcast.10, bf16[48,6,2,128]{3,2,1,0:T(2,128)(2,1)S(1)} %collective-permute-done.2), kind=kLoop, calls=%fused_computation.35 | loop fusion | flops 5308416 | bytes 4423680 | tf_op jit(solution)/shard_map/slice | solution.py:20
  36.9 0.2 copy.5
  37.2 1.8 %collective-permute-start.4 = (bf16[48,2,36,128]{3,0,2,1:T(8,128)(2,1)S(1)}, bf16[48,2,36,128]{3,0,2,1:T(8,128)(2,1)S(1)}, u32[]{:S(2)}, u32[]{:S(2)}) collective-permute-start(bf16[48,2,36,128]{3,0,2,1:T(8,128)(2,1)S(1)} %copy.5), channel_id=1, source_target_pairs={{0,1},{1,2},{2,3},{3,0},{4,5},{5,6},{6,7},{7,4},{8,9},{9,10},{10,1... | collective-permute-start | bytes 2654216 | tf_op jit(solution)/shard_map/ppermute | solution.py:22
  39.0 0.2 copy.6
  39.2 0.0 collective-permute-done.10
  39.2 0.1 collective-permute-start.5
  39.3 0.0 collective-permute-done.11
  39.3 0.3 pad_maximum_fusion.7
  39.6 1.8 %collective-permute-start.12 = (bf16[15,2,36,128]{3,2,1,0:T(8,128)(2,1)S(1)}, bf16[15,2,36,128]{3,2,1,0:T(8,128)(2,1)S(1)}, u32[]{:S(2)}, u32[]{:S(2)}) collective-permute-start(bf16[15,2,36,128]{3,2,1,0:T(8,128)(2,1)S(1)} %get-tuple-element.11), channel_id=1, source_target_pairs={{0,1},{1,2},{2,3},{3,0},{4,5},{5,6},{6,7},{7,4},{8,9},{9,10},{10,1... | collective-permute-start | bytes 829448 | tf_op jit(solution)/shard_map/ppermute | solution.py:22
  41.4 0.0 collective-permute-done.8
  41.4 0.0 collective-permute-start.13
  41.4 0.3 collective-permute-done.9
  41.8 1.3 %select_maximum_fusion.4.pres_ref = bf16[8,10,48,128]{3,2,1,0:T(8,128)(2,1)} fusion(bf16[8,2,36,128]{3,2,1,0:T(8,128)(2,1)S(1)} %collective-permute-done.9, bf16[8,2,36,128]{3,2,1,0:T(8,128)(2,1)S(1)} %collective-permute-done.8, bf16[8,6,2,128]{3,2,1,0:T(2,128)(2,1)S(1)} %collective-permute-done.7, bf16[8,6,32,128]{3,2,1,0:T(8,128)(2,1)S(1)} %bitcast.20, ...), kind=kLoop, calls=%fused_computation.26 | loop fusion | flops 8847360 | bytes 1720320 | tf_op jit(solution)/shard_map/concatenate | solution.py:24
  43.1 20.3 %collective-permute-done.12 = bf16[15,2,36,128]{3,2,1,0:T(8,128)(2,1)S(1)} collective-permute-done((bf16[15,2,36,128]{3,2,1,0:T(8,128)(2,1)S(1)}, bf16[15,2,36,128]{3,2,1,0:T(8,128)(2,1)S(1)}, u32[]{:S(2)}, u32[]{:S(2)}) %collective-permute-start.12) | collective-permute-done | bytes 276512 | tf_op jit(solution)/shard_map/ppermute | solution.py:22
  63.4 3.4 %collective-permute-done.13 = bf16[15,2,36,128]{3,2,1,0:T(8,128)(2,1)S(1)} collective-permute-done((bf16[15,2,36,128]{3,2,1,0:T(8,128)(2,1)S(1)}, bf16[15,2,36,128]{3,2,1,0:T(8,128)(2,1)S(1)}, u32[]{:S(2)}, u32[]{:S(2)}) %collective-permute-start.13) | collective-permute-done | bytes 276512 | tf_op jit(solution)/shard_map/ppermute | solution.py:23
  66.8 2.8 %select_maximum_fusion.2.base_ref = bf16[15,10,48,128]{3,2,1,0:T(8,128)(2,1)} fusion(bf16[15,2,36,128]{3,2,1,0:T(8,128)(2,1)S(1)} %collective-permute-done.13, bf16[15,2,36,128]{3,2,1,0:T(8,128)(2,1)S(1)} %collective-permute-done.12, bf16[15,6,2,128]{3,2,1,0:T(2,128)(2,1)S(1)} %collective-permute-done.11, ...), kind=kLoop, calls=%fused_computation.17 | loop fusion | flops 19353600 | bytes 3225600 | tf_op jit(solution)/shard_map/concatenate | solution.py:24
  69.7 0.0 collective-permute-done.4
  69.7 0.2 copy.7
  69.9 0.0 collective-permute-done.5
  69.9 0.2 copy.8
  70.2 4.1 %select_maximum_fusion.vel_ref = bf16[48,10,48,128]{3,2,1,0:T(8,128)(2,1)} fusion(bf16[48,2,36,128]{3,2,1,0:T(8,128)(2,1)S(1)} %copy.8, bf16[48,2,36,128]{3,2,1,0:T(8,128)(2,1)S(1)} %copy.7, bf16[48,6,2,128]{3,2,1,0:T(2,128)(2,1)S(1)} %collective-permute-done.3, bf16[48,6,32,128]{3,2,1,0:T(8,128)(2,1)S(1)} %bitcast.11, ...), kind=kLoop, calls=%fused_computation.3 | loop fusion | flops 53084160 | bytes 10321920 | tf_op jit(solution)/shard_map/concatenate | solution.py:24
  74.3 24.2 %shard_map.46 = f32[4,2,4,6,32,128]{5,4,3,2,1,0:T(8,128)} custom-call(bf16[48,10,48,128]{3,2,1,0:T(8,128)(2,1)} %select_maximum_fusion.vel_ref, bf16[8,10,48,128]{3,2,1,0:T(8,128)(2,1)} %select_maximum_fusion.4.pres_ref, bf16[15,10,48,128]{3,2,1,0:T(8,128)(2,1)} %select_maximum_fusion.2.base_ref, s32[6,32,128]{2,1,0:T(8,128)} %bitcast.24), custom_call_target="tpu_custom_call" | custom-call | tf_op jit(solution)/shard_map/pallas_call | solution.py:179
  (4 shorter events, 0.1 us)
Async XLA Ops:
  0.0 7.8 %copy-start.1 = (bf16[4,2,4,32,6,128]{5,3,4,2,1,0:T(8,128)(2,1)S(1)}, bf16[4,2,4,32,6,128]{5,3,4,2,1,0:T(8,128)(2,1)}, u32[]{:S(2)}) copy-start(bf16[4,2,4,32,6,128]{5,3,4,2,1,0:T(8,128)(2,1)} %param.4) | copy-start | bytes 4718596
  1.6 16.3 %collective-permute-start = (bf16[2,2,3,6,32,128]{5,4,3,2,1,0:T(8,128)(2,1)S(1)}, bf16[2,2,3,6,32,128]{5,4,3,2,1,0:T(8,128)(2,1)S(1)}, u32[]{:S(2)}, u32[]{:S(2)}) collective-permute-start(bf16[2,2,3,6,32,128]{5,4,3,2,1,0:T(8,128)(2,1)S(1)} %get-tuple-element.9), channel_id=1, source_target_pairs={{0,16},{16,32},{32,48},{48,64},{64,80},{80,96},{96,112},{1,17},{17... | collective-permute-start | bytes 1769480 | tf_op jit(solution)/shard_map/ppermute | solution.py:22
  5.9 19.4 %collective-permute-start.1 = (bf16[2,2,3,6,32,128]{5,4,3,2,1,0:T(8,128)(2,1)S(1)}, bf16[2,2,3,6,32,128]{5,4,3,2,1,0:T(8,128)(2,1)S(1)}, u32[]{:S(2)}, u32[]{:S(2)}) collective-permute-start(bf16[2,2,3,6,32,128]{5,4,3,2,1,0:T(8,128)(2,1)S(1)} %get-tuple-element.10), channel_id=1, source_target_pairs={{16,0},{32,16},{48,32},{64,48},{80,64},{96,80},{112,96},{17,1},{33... | collective-permute-start | bytes 1769480 | tf_op jit(solution)/shard_map/ppermute | solution.py:23
  7.9 22.0 %collective-permute-start.6 = (bf16[8,6,2,128]{3,2,1,0:T(2,128)(2,1)S(1)}, bf16[8,6,2,128]{3,2,1,0:T(2,128)(2,1)S(1)}, u32[]{:S(2)}, u32[]{:S(2)}) collective-permute-start(bf16[8,6,2,128]{3,2,1,0:T(2,128)(2,1)S(1)} %get-tuple-element.17), channel_id=1, source_target_pairs={{0,4},{4,8},{8,12},{12,0},{1,5},{5,9},{9,13},{13,1},{2,6},{6,10},{... | collective-permute-start | bytes 73736 | tf_op jit(solution)/shard_map/ppermute | solution.py:22
  9.6 23.0 %collective-permute-start.7 = (bf16[8,6,2,128]{3,2,1,0:T(2,128)(2,1)S(1)}, bf16[8,6,2,128]{3,2,1,0:T(2,128)(2,1)S(1)}, u32[]{:S(2)}, u32[]{:S(2)}) collective-permute-start(bf16[8,6,2,128]{3,2,1,0:T(2,128)(2,1)S(1)} %get-tuple-element.18), channel_id=1, source_target_pairs={{4,0},{8,4},{12,8},{0,12},{5,1},{9,5},{13,9},{1,13},{6,2},{10,6},{... | collective-permute-start | bytes 73736 | tf_op jit(solution)/shard_map/ppermute | solution.py:23
  12.0 17.7 %copy-start = (bf16[2,2,3,32,6,128]{5,3,4,2,1,0:T(8,128)(2,1)S(1)}, bf16[2,2,3,32,6,128]{5,3,4,2,1,0:T(8,128)(2,1)}, u32[]{:S(2)}) copy-start(bf16[2,2,3,32,6,128]{5,3,4,2,1,0:T(8,128)(2,1)} %param.6) | copy-start | bytes 1769476
  12.0 17.7 %copy-start.2 = (bf16[3,32,6,128]{3,1,2,0:T(8,128)(2,1)S(1)}, bf16[3,32,6,128]{3,1,2,0:T(8,128)(2,1)}, u32[]{:S(2)}) copy-start(bf16[3,32,6,128]{3,1,2,0:T(8,128)(2,1)} %param.5) | copy-start | bytes 442372
  25.8 9.8 %collective-permute-start.2 = (bf16[48,6,2,128]{3,2,1,0:T(2,128)(2,1)S(1)}, bf16[48,6,2,128]{3,2,1,0:T(2,128)(2,1)S(1)}, u32[]{:S(2)}, u32[]{:S(2)}) collective-permute-start(bf16[48,6,2,128]{3,2,1,0:T(2,128)(2,1)S(1)} %get-tuple-element.7), channel_id=1, source_target_pairs={{0,4},{4,8},{8,12},{12,0},{1,5},{5,9},{9,13},{13,1},{2,6},{6,10},{... | collective-permute-start | bytes 442376 | tf_op jit(solution)/shard_map/ppermute | solution.py:22
  27.6 8.1 %collective-permute-start.3 = (bf16[48,6,2,128]{3,2,1,0:T(2,128)(2,1)S(1)}, bf16[48,6,2,128]{3,2,1,0:T(2,128)(2,1)S(1)}, u32[]{:S(2)}, u32[]{:S(2)}) collective-permute-start(bf16[48,6,2,128]{3,2,1,0:T(2,128)(2,1)S(1)} %get-tuple-element.8), channel_id=1, source_target_pairs={{4,0},{8,4},{12,8},{0,12},{5,1},{9,5},{13,9},{1,13},{6,2},{10,6},{... | collective-permute-start | bytes 442376 | tf_op jit(solution)/shard_map/ppermute | solution.py:23
  29.8 9.4 %collective-permute-start.10 = (bf16[15,6,2,128]{3,2,1,0:T(2,128)(2,1)S(1)}, bf16[15,6,2,128]{3,2,1,0:T(2,128)(2,1)S(1)}, u32[]{:S(2)}, u32[]{:S(2)}) collective-permute-start(bf16[15,6,2,128]{3,2,1,0:T(2,128)(2,1)S(1)} %get-tuple-element.13), channel_id=1, source_target_pairs={{0,4},{4,8},{8,12},{12,0},{1,5},{5,9},{9,13},{13,1},{2,6},{6,10},{... | collective-permute-start | bytes 138248 | tf_op jit(solution)/shard_map/ppermute | solution.py:22
  29.9 9.4 %collective-permute-start.11 = (bf16[15,6,2,128]{3,2,1,0:T(2,128)(2,1)S(1)}, bf16[15,6,2,128]{3,2,1,0:T(2,128)(2,1)S(1)}, u32[]{:S(2)}, u32[]{:S(2)}) collective-permute-start(bf16[15,6,2,128]{3,2,1,0:T(2,128)(2,1)S(1)} %get-tuple-element.14), channel_id=1, source_target_pairs={{4,0},{8,4},{12,8},{0,12},{5,1},{9,5},{13,9},{1,13},{6,2},{10,6},{... | collective-permute-start | bytes 138248 | tf_op jit(solution)/shard_map/ppermute | solution.py:23
  32.7 8.7 %collective-permute-start.8 = (bf16[8,2,36,128]{3,2,1,0:T(8,128)(2,1)S(1)}, bf16[8,2,36,128]{3,2,1,0:T(8,128)(2,1)S(1)}, u32[]{:S(2)}, u32[]{:S(2)}) collective-permute-start(bf16[8,2,36,128]{3,2,1,0:T(8,128)(2,1)S(1)} %get-tuple-element.15), channel_id=1, source_target_pairs={{0,1},{1,2},{2,3},{3,0},{4,5},{5,6},{6,7},{7,4},{8,9},{9,10},{10,1... | collective-permute-start | bytes 442376 | tf_op jit(solution)/shard_map/ppermute | solution.py:22
  35.7 6.1 %collective-permute-start.9 = (bf16[8,2,36,128]{3,2,1,0:T(8,128)(2,1)S(1)}, bf16[8,2,36,128]{3,2,1,0:T(8,128)(2,1)S(1)}, u32[]{:S(2)}, u32[]{:S(2)}) collective-permute-start(bf16[8,2,36,128]{3,2,1,0:T(8,128)(2,1)S(1)} %get-tuple-element.16), channel_id=1, source_target_pairs={{1,0},{2,1},{3,2},{0,3},{5,4},{6,5},{7,6},{4,7},{9,8},{10,9},{11,1... | collective-permute-start | bytes 442376 | tf_op jit(solution)/shard_map/ppermute | solution.py:23
  37.2 32.5 %collective-permute-start.4 = (bf16[48,2,36,128]{3,0,2,1:T(8,128)(2,1)S(1)}, bf16[48,2,36,128]{3,0,2,1:T(8,128)(2,1)S(1)}, u32[]{:S(2)}, u32[]{:S(2)}) collective-permute-start(bf16[48,2,36,128]{3,0,2,1:T(8,128)(2,1)S(1)} %copy.5), channel_id=1, source_target_pairs={{0,1},{1,2},{2,3},{3,0},{4,5},{5,6},{6,7},{7,4},{8,9},{9,10},{10,1... | collective-permute-start | bytes 2654216 | tf_op jit(solution)/shard_map/ppermute | solution.py:22
  39.2 30.7 %collective-permute-start.5 = (bf16[48,2,36,128]{3,0,2,1:T(8,128)(2,1)S(1)}, bf16[48,2,36,128]{3,0,2,1:T(8,128)(2,1)S(1)}, u32[]{:S(2)}, u32[]{:S(2)}) collective-permute-start(bf16[48,2,36,128]{3,0,2,1:T(8,128)(2,1)S(1)} %copy.6), channel_id=1, source_target_pairs={{1,0},{2,1},{3,2},{0,3},{5,4},{6,5},{7,6},{4,7},{9,8},{10,9},{11,1... | collective-permute-start | bytes 2654216 | tf_op jit(solution)/shard_map/ppermute | solution.py:23
  39.6 23.8 %collective-permute-start.12 = (bf16[15,2,36,128]{3,2,1,0:T(8,128)(2,1)S(1)}, bf16[15,2,36,128]{3,2,1,0:T(8,128)(2,1)S(1)}, u32[]{:S(2)}, u32[]{:S(2)}) collective-permute-start(bf16[15,2,36,128]{3,2,1,0:T(8,128)(2,1)S(1)} %get-tuple-element.11), channel_id=1, source_target_pairs={{0,1},{1,2},{2,3},{3,0},{4,5},{5,6},{6,7},{7,4},{8,9},{9,10},{10,1... | collective-permute-start | bytes 829448 | tf_op jit(solution)/shard_map/ppermute | solution.py:22
  41.4 25.4 %collective-permute-start.13 = (bf16[15,2,36,128]{3,2,1,0:T(8,128)(2,1)S(1)}, bf16[15,2,36,128]{3,2,1,0:T(8,128)(2,1)S(1)}, u32[]{:S(2)}, u32[]{:S(2)}) collective-permute-start(bf16[15,2,36,128]{3,2,1,0:T(8,128)(2,1)S(1)} %get-tuple-element.12), channel_id=1, source_target_pairs={{1,0},{2,1},{3,2},{0,3},{5,4},{6,5},{7,6},{4,7},{9,8},{10,9},{11,1... | collective-permute-start | bytes 829448 | tf_op jit(solution)/shard_map/ppermute | solution.py:23
where the time goes:
time: 98.7 us; the launch traced here: 98.5 us
  waiting for transfers between devices  37.4 us (38%)
  Pallas kernels  24.2 us (25%)
  starting transfers between devices  23.4 us (24%)
  other arithmetic  10.3 us (10%)
  local copies, waits for them, and re-layouts  3.03 us (3%)
    ppermute x7, waiting for transfers between devices, with_halo(): before = lax.ppermute(last, axis, up)  26.1 us
    pallas_call x1, Pallas kernels, shards(): pl.pallas_call(kernel, out_shape=jax.ShapeDtypeStruct((per, 2, 4, cz, cx,...  24.2 us
    ppermute x7, starting transfers between devices, with_halo(): before = lax.ppermute(last, axis, up)  14.3 us
    ppermute x7, waiting for transfers between devices, with_halo(): after = lax.ppermute(first, axis, down)  11.2 us
    ppermute x7, starting transfers between devices, with_halo(): after = lax.ppermute(first, axis, down)  9.06 us
    concatenate x4, other arithmetic, with_halo(): shard = jnp.concatenate([before, shard, after], axis=dim)  8.55 us
    slice x4, local copies, waits for them, and re-layouts, with_halo(): last = lax.slice_in_dim(shard, length - width, length, axis=dim)  2.07 us
  transfers between devices with their start and end apart: 14, of which 5 were waited for; matrix products, arithmetic and copies ran while one was open for 8% of the time, Pallas kernels for 0%

commit v1 on v0

v1 whole, which is shorter than its diff:
```python
import jax
import jax.numpy as jnp
from jax import lax
from jax.experimental import pallas as pl
from jax.experimental.pallas import tpu as pltpu
from jax.sharding import PartitionSpec as P

FREQUENCY_STEP = 0.2
VISCOSITY = 0.05
PENALTY = 4.0
TWELFTH = 1.0 / 12.0
MESH = pl.DeviceIdType.MESH

LAYERS, ROWS, LANES = 10, 48, 128
OWN_Z = pl.ds(2, 6)
OWN_X = pl.ds(8, 32)
RIM_Z = {1: pl.ds(0, 2), -1: pl.ds(8, 2)}
RIM_X = {1: pl.ds(6, 2), -1: pl.ds(40, 2)}
BARE_Z = {1: pl.ds(4, 2), -1: pl.ds(0, 2)}
BARE_X = {1: pl.ds(30, 2), -1: pl.ds(0, 2)}
SLAB_Z = {1: pl.ds(6, 2), -1: pl.ds(2, 2)}
SLAB_X = {1: pl.ds(38, 2), -1: pl.ds(8, 2)}

OWN0, LOW0, HIGH0, BASE0, FIELDS = 0, 32, 44, 56, 71


def vel(l, part, c):
    if l < 0:
        return LOW0 + ((l + 2) * 2 + part) * 3 + c
    if l > 3:
        return HIGH0 + ((l - 4) * 2 + part) * 3 + c
    return OWN0 + (l * 2 + part) * 4 + c


def base(m, part, c):
    return BASE0 + (c if m == 0 else 3 + ((m - 1) * 2 + part) * 3 + c)


MODES = [(0, 0), (1, 0), (1, 1), (2, 0), (2, 1)]
OWN = (0, 1, 2, 3)
OTHERS = (-2, -1, 4, 5)


def block(slabs, mask, out, masks, freqs, z, xb, jobs, first):
    row = xb * 8 + 8
    here = pl.ds(xb * 8, 8)

    def load(field, dz=0, dx=0):
        return slabs[field, z + 2 + dz, pl.ds(row + dx, 8), :]

    def lane(value, offset):
        return jnp.where(masks[offset], pltpu.roll(value, (-offset) % LANES, 1), 0.0)

    def sides(field, d):
        if d == 0:
            return tuple(load(field, 0, o) for o in (1, -1, 2, -2))
        if d == 2:
            return tuple(load(field, o, 0) for o in (1, -1, 2, -2))
        value = load(field)
        return tuple(lane(value, o) for o in (1, -1, 2, -2))

    def slope(s):
        return 8.0 * (s[0] - s[1]) - (s[2] - s[3])

    used = sorted({d for _, dirs in jobs for d in dirs})
    flow = {(m, part, d): load(base(m, part, d)) * TWELFTH for m, part in MODES for d in used}
    solid = PENALTY * mask[z, here, :].astype(jnp.float32) if first else None
    diverge = {}
    for c in range(3):
        bend = {(m, part, d): slope(sides(base(m, part, c), d)) * TWELFTH for m, part in MODES for d in used}
        total = {}
        if not first:
            total = {(k, part): out[k, part, c, z, here, :] for k in OWN for part in range(2)}

        def add(key, term):
            total[key] = total[key] + term if key in total else term

        def sub(key, term):
            total[key] = total[key] - term if key in total else -term

        for ls, dirs in jobs:
            for l in ls:
                grad = {}
                for part in range(2):
                    around = {d: sides(vel(l, part, c), d) for d in dirs}
                    for d in dirs:
                        grad[part, d] = slope(around[d])
                    if l in OWN:
                        key = (l, part)
                        near = sum(around[d][0] + around[d][1] for d in dirs)
                        far = sum(around[d][2] + around[d][3] for d in dirs)
                        sub(key, (VISCOSITY * 16.0 * TWELFTH) * near)
                        add(key, (VISCOSITY * TWELFTH) * far)
                        if 0 in dirs:
                            value = load(vel(l, part, c))
                            add(key, (solid + VISCOSITY * 90.0 * TWELFTH) * value)
                            turn = freqs[l] * load(vel(l, 1 - part, c))
                            (sub if part == 0 else add)(key, turn)
                        if c in dirs:
                            add(key, slope(sides(OWN0 + (l * 2 + part) * 4 + 3, c)) * TWELFTH)
                            diverge[key] = diverge[key] + grad[part, c] if key in diverge else grad[part, c]
                speed = {(part, d): load(vel(l, part, d)) for part in range(2) for d in dirs}
                for k in OWN:
                    m = k - l
                    if abs(m) > 2:
                        continue
                    a = abs(m)
                    for d in dirs:
                        gr, gi = grad[0, d], grad[1, d]
                        ur, ui = speed[0, d], speed[1, d]
                        fr, br = flow[a, 0, d], bend[a, 0, d]
                        add((k, 0), fr * gr + ur * br)
                        add((k, 1), fr * gi + ui * br)
                        if a:
                            fi, bi = flow[a, 1, d], bend[a, 1, d]
                            real, imag = fi * gi + ui * bi, fi * gr + ur * bi
                            (sub if m > 0 else add)((k, 0), real)
                            (add if m > 0 else sub)((k, 1), imag)
        for key, value in total.items():
            out[key[0], key[1], c, z, here, :] = value
    for (k, part), value in diverge.items():
        value = value * TWELFTH
        out[k, part, 3, z, here, :] = value if first else out[k, part, 3, z, here, :] + value


def kernel(pert, mean, modes, solid_hbm, out_hbm, own, low, high, flow, slabs, out, solid, local_sem, send_sem, recv_sem, out_sem):
    h, gx, gz = lax.axis_index("harm"), lax.axis_index("gx"), lax.axis_index("gz")
    side_x = {1: lax.rem(gx + 1, 4), -1: lax.rem(gx + 3, 4)}
    side_z = {1: lax.rem(gz + 1, 4), -1: lax.rem(gz + 3, 4)}
    odd = lax.rem(gz, 2)
    twin = {1: lax.rem(h + 4 * odd, 8), -1: lax.rem(h + 4 * (1 - odd), 8)}
    has_low, has_high = h > 0, h < 7

    barrier = pltpu.get_barrier_semaphore()

    def greet(device):
        pl.semaphore_signal(barrier, inc=1, device_id=device, device_id_type=MESH)

    for s in (1, -1):
        greet((h, side_x[s], gz))
        greet((h, gx, side_z[s]))
    greet((lax.rem(h + 4, 8), gx, 3 - gz))

    @pl.when(has_low)
    def _():
        greet((h - 1, gx, gz))

    @pl.when(has_high)
    def _():
        greet((h + 1, gx, gz))

    def local(i, src, dst):
        return pltpu.make_async_copy(src, dst, local_sem.at[i])

    loads = [
        local(0, pert, own.at[:, :, :, OWN_Z, OWN_X]),
        local(1, mean, flow.at[pl.ds(0, 3), OWN_Z, OWN_X]),
        local(2, modes.at[0, 0], flow.at[pl.ds(3, 3), OWN_Z, OWN_X]),
        local(3, modes.at[0, 1], flow.at[pl.ds(6, 3), OWN_Z, OWN_X]),
        local(4, modes.at[1, 0], flow.at[pl.ds(9, 3), OWN_Z, OWN_X]),
        local(5, modes.at[1, 1], flow.at[pl.ds(12, 3), OWN_Z, OWN_X]),
        local(6, solid_hbm, solid),
    ]
    for copy in loads:
        copy.start()

    pl.semaphore_wait(barrier, 5 + jnp.where(has_low, 1, 0) + jnp.where(has_high, 1, 0))

    counter = iter(range(64))

    def remote(src, dst, device):
        i = next(counter)
        return pltpu.make_async_remote_copy(
            src_ref=src, dst_ref=dst, send_sem=send_sem.at[i], recv_sem=recv_sem.at[i], device_id=device, device_id_type=MESH
        )

    three = pl.ds(0, 3)
    tile = (slice(None), slice(None), slice(None), OWN_Z, OWN_X)
    up = remote(pert.at[pl.ds(2, 2), :, three], low.at[tile], (jnp.minimum(h + 1, 7), gx, gz))
    down = remote(pert.at[pl.ds(0, 2), :, three], high.at[tile], (jnp.maximum(h - 1, 0), gx, gz))
    rim_x, rim_z, base_x, base_z = [], [], [], []
    for s in (1, -1):
        rim_z.append(remote(pert.at[:, :, :, BARE_Z[s]], own.at[:, :, :, RIM_Z[s], OWN_X], (h, gx, side_z[s])))
        rim_x.append(remote(pert.at[:, :, :, :, BARE_X[s]], own.at[:, :, :, OWN_Z, RIM_X[s]], (h, side_x[s], gz)))
        pieces = [(mean, 0)] + [(modes.at[m, part], 3 + (m * 2 + part) * 3) for m in range(2) for part in range(2)]
        for ref, at in pieces:
            fields = pl.ds(at, 3)
            base_x.append(remote(ref.at[:, :, BARE_X[s]], flow.at[fields, OWN_Z, RIM_X[s]], (h, side_x[s], gz)))
            base_z.append(remote(ref.at[:, BARE_Z[s]], flow.at[fields, RIM_Z[s], OWN_X], (twin[s], gx, side_z[s])))
    pl.when(has_high)(up.start)
    pl.when(has_low)(down.start)
    for copy in rim_x + rim_z + base_x + base_z:
        copy.start()
    corner = {}
    for name, ref in (("low", low), ("high", high)):
        corner[name, "x"] = [
            remote(ref.at[:, :, :, OWN_Z, SLAB_X[s]], ref.at[:, :, :, OWN_Z, RIM_X[s]], (h, side_x[s], gz)) for s in (1, -1)
        ]
        corner[name, "z"] = [
            remote(ref.at[:, :, :, SLAB_Z[s], OWN_X], ref.at[:, :, :, RIM_Z[s], OWN_X], (h, gx, side_z[s])) for s in (1, -1)
        ]

    def stage(ref, shape, first, layers, rows):
        def body(i, carry):
            index, rest = [], i
            for size in reversed(shape):
                index.insert(0, lax.rem(rest, size))
                rest = lax.div(rest, size)
            for z in layers:
                slabs[first + i, z, rows, :] = ref[(*index, z, rows)].astype(jnp.float32)
            return carry

        count = 1
        for size in shape:
            count *= size
        lax.fori_loop(0, count, body, 0)

    middle, edge = range(2, 8), (0, 1, 8, 9)
    every = pl.ds(0, ROWS)
    for copy in loads:
        copy.wait()
    for copy in rim_x + base_x:
        copy.wait_recv()
    stage(own, (4, 2, 4), OWN0, middle, every)
    stage(flow, (15,), BASE0, middle, every)

    lanes = lax.broadcasted_iota(jnp.int32, (8, LANES), 1)
    masks = {1: lanes < LANES - 1, 2: lanes < LANES - 2, -1: lanes >= 1, -2: lanes >= 2}
    freqs = [FREQUENCY_STEP * (h * 4 + k - 16).astype(jnp.float32) for k in range(4)]

    def sweep(jobs, first, finish=None):
        def layer(z, carry):
            def chunk(xb, inner):
                block(slabs, solid, out, masks, freqs, z, xb, jobs, first)
                return inner

            lax.fori_loop(0, 4, chunk, 0)
            if finish is not None:
                finish(z)
            return carry

        lax.fori_loop(0, 6, layer, 0)

    sweep([(OWN, (0, 1))], True)

    def relay(present, ref, name, arrival, first):
        @pl.when(present)
        def _():
            arrival.wait_recv()
            for copy in corner[name, "z"] + corner[name, "x"]:
                copy.start()

    relay(has_low, low, "low", up, LOW0)
    relay(has_high, high, "high", down, HIGH0)
    for copy in rim_z + base_z:
        copy.wait_recv()
    stage(own, (4, 2, 4), OWN0, edge, OWN_X)
    stage(flow, (15,), BASE0, edge, OWN_X)
    sweep([(OWN, (2,))], False)

    def settle(present, ref, name, first):
        @pl.when(present)
        def _():
            for copy in corner[name, "z"] + corner[name, "x"]:
                copy.wait_recv()
            stage(ref, (2, 2, 3), first, middle, every)
            stage(ref, (2, 2, 3), first, edge, OWN_X)

        @pl.when(jnp.logical_not(present))
        def _():
            def clear(i, carry):
                slabs[first + i] = jnp.zeros((LAYERS, ROWS, LANES), jnp.float32)
                return carry

            lax.fori_loop(0, 12, clear, 0)

    settle(has_low, low, "low", LOW0)
    settle(has_high, high, "high", HIGH0)

    def write(z):
        return pltpu.make_async_copy(out.at[:, :, :, z], out_hbm.at[:, :, :, z], out_sem.at[z])

    sweep([(OTHERS, (0, 1, 2))], False, lambda z: write(z).start())

    def drain(z, carry):
        write(z).wait()
        return carry

    lax.fori_loop(0, 6, drain, 0)
    for copy in rim_x + rim_z + base_x + base_z:
        copy.wait_send()
    pl.when(has_high)(up.wait_send)
    pl.when(has_low)(down.wait_send)
    for present, name in ((has_low, "low"), (has_high, "high")):

        @pl.when(present)
        def _(name=name):
            for copy in corner[name, "z"] + corner[name, "x"]:
                copy.wait_send()


def shards(perturbation, base_mean, base_modes, solid_mask):
    turned = jnp.transpose(perturbation, (0, 1, 2, 4, 3, 5))
    mean = jnp.transpose(base_mean, (0, 2, 1, 3))
    modes = jnp.transpose(base_modes, (0, 1, 2, 4, 3, 5))
    mask = jnp.transpose(solid_mask, (1, 0, 2))
    anywhere = pl.BlockSpec(memory_space=pl.ANY)
    half = jnp.bfloat16
    out = pl.pallas_call(
        kernel,
        out_shape=jax.ShapeDtypeStruct(turned.shape, jnp.float32),
        in_specs=[anywhere] * 4,
        out_specs=anywhere,
        scratch_shapes=[
            pltpu.VMEM((4, 2, 4, LAYERS, ROWS, LANES), half),
            pltpu.VMEM((2, 2, 3, LAYERS, ROWS, LANES), half),
            pltpu.VMEM((2, 2, 3, LAYERS, ROWS, LANES), half),
            pltpu.VMEM((15, LAYERS, ROWS, LANES), half),
            pltpu.VMEM((FIELDS, LAYERS, ROWS, LANES), jnp.float32),
            pltpu.VMEM(turned.shape, jnp.float32),
            pltpu.VMEM(mask.shape, jnp.int32),
            pltpu.SemaphoreType.DMA((7,)),
            pltpu.SemaphoreType.DMA((34,)),
            pltpu.SemaphoreType.DMA((34,)),
            pltpu.SemaphoreType.DMA((6,)),
        ],
        compiler_params=pltpu.CompilerParams(collective_id=0, has_side_effects=True, vmem_limit_bytes=60 * 1024 * 1024),
    )(turned, mean, modes, mask)
    return jnp.transpose(out, (0, 1, 2, 4, 3, 5))


def solution(mesh):
    return jax.shard_map(
        shards,
        mesh=mesh,
        in_specs=(
            P("harm", None, None, "gx", "gz", None),
            P(None, "gx", "gz", None),
            P(None, None, None, "gx", "gz", None),
            P("gx", "gz", None),
        ),
        out_specs=P("harm", None, None, "gx", "gz", None),
        check_vma=False,
    )
```

time: 98.7 us -> 51.7 us (0.52)
  waiting for transfers between devices: 37.4 us -> 0 us
  starting transfers between devices: 23.4 us -> 0 us
  Pallas kernels: 24.2 us -> 47.5 us
  other arithmetic: 10.3 us -> 0 us
  local copies, waits for them, and re-layouts: 3.03 us -> 4.05 us
    ppermute x14 -> x0, waiting for transfers between devices: 37.4 us -> none  [the longest x7 26.1 us: with_halo(): before = lax.ppermute(last, axis, up)]
    ppermute x14 -> x0, starting transfers between devices: 23.4 us -> none  [the longest x7 14.3 us: with_halo(): before = lax.ppermute(last, axis, up)]
    pallas_call x1, Pallas kernels: 24.2 us -> 47.5 us  [shards(): pl.pallas_call(kernel, out_shape=jax.ShapeDtypeStruct(turned.shape, jnp.f...]
    concatenate x4 -> x0, other arithmetic: 8.55 us -> none  [with_halo(): shard = jnp.concatenate([before, shard, after], axis=dim)]
    unnamed x6 -> x1, local copies, waits for them, and re-layouts: 0.02 us -> 4.05 us
    slice x7 -> x0, local copies, waits for them, and re-layouts: 2.53 us -> none  [the longest x4 2.07 us: with_halo(): last = lax.slice_in_dim(shard, length - width, length, axis=dim)]
    slice x4 -> x0, other arithmetic: 1.78 us -> none  [with_halo(): last = lax.slice_in_dim(shard, length - width, length, axis=dim)]
  transfers between devices with their start and end apart: 14 -> 0, of which waited for: 5 -> 0; matrix products, arithmetic and copies ran while one was open for 8% -> 0% of each run, Pallas kernels for 0% -> 0%
where the time goes in v1:
time: 51.7 us; the launch traced here: 51.6 us
  Pallas kernels  47.5 us (92%)
  local copies, waits for them, and re-layouts  4.05 us (8%)
    pallas_call x1, Pallas kernels, shards(): pl.pallas_call(kernel, out_shape=jax.ShapeDtypeStruct(turned.shape, jnp.f...  47.5 us
    unnamed x1, local copies, waits for them, and re-layouts  4.05 us

profile of v1, /device:TPU:25, one launch (start us, length us, event | category | flops | bytes accessed | tf_op | source)
XLA Modules:
  0.0 51.6 jit_solution(731816908301355162)
XLA Ops:
  0.0 47.5 %shard_map.46 = f32[4,2,4,6,32,128]{5,4,3,2,1,0:T(8,128)} custom-call(bf16[4,2,4,6,32,128]{5,4,3,2,1,0:T(8,128)(2,1)} %bitcast.6, bf16[3,6,32,128]{3,2,1,0:T(8,128)(2,1)} %bitcast.8, bf16[2,2,3,6,32,128]{5,4,3,2,1,0:T(8,128)(2,1)} %bitcast.7, s32[6,32,128]{2,1,0:T(8,128)} %bitcast.9), custom_call_target="tpu_custom_call" | custom-call | tf_op jit(solution)/shard_map/pallas_call | solution.py:309
  47.5 4.0 %copy.6 = f32[4,2,4,32,6,128]{5,3,4,2,1,0:T(8,128)} copy(f32[4,2,4,32,6,128]{5,3,4,2,1,0:T(8,128)} %bitcast.5) | data formatting | bytes 6291456

commit v2 on v1

--- a/solution.py
+++ b/solution.py
@@ -63,11 +63,11 @@
         return 8.0 * (s[0] - s[1]) - (s[2] - s[3])
 
     used = sorted({d for _, dirs in jobs for d in dirs})
-    flow = {(m, part, d): load(base(m, part, d)) * TWELFTH for m, part in MODES for d in used}
+    flow = {(m, part, d): load(base(m, part, d)) for m, part in MODES for d in used}
     solid = PENALTY * mask[z, here, :].astype(jnp.float32) if first else None
     diverge = {}
     for c in range(3):
-        bend = {(m, part, d): slope(sides(base(m, part, c), d)) * TWELFTH for m, part in MODES for d in used}
+        bend = {(m, part, d): slope(sides(base(m, part, c), d)) for m, part in MODES for d in used}
         total = {}
         if not first:
             total = {(k, part): out[k, part, c, z, here, :] for k in OWN for part in range(2)}
@@ -141,6 +141,20 @@
         greet((h, gx, side_z[s]))
     greet((lax.rem(h + 4, 8), gx, 3 - gz))
 
+    bent, across = odd == 1, lax.rem(gz + 2, 4)
+    inner = jnp.logical_or(h == 3, h == 4)
+    outer = jnp.logical_or(h == 0, h == 7)
+
+    @pl.when(bent & inner)
+    def _():
+        greet((0, gx, across))
+        greet((7, gx, across))
+
+    @pl.when(bent & outer)
+    def _():
+        greet((3, gx, across))
+        greet((4, gx, across))
+
     @pl.when(has_low)
     def _():
         greet((h - 1, gx, gz))
@@ -164,7 +178,8 @@
     for copy in loads:
         copy.start()
 
-    pl.semaphore_wait(barrier, 5 + jnp.where(has_low, 1, 0) + jnp.where(has_high, 1, 0))
+    extra = jnp.where(bent & jnp.logical_or(inner, outer), 2, 0)
+    pl.semaphore_wait(barrier, 5 + jnp.where(has_low, 1, 0) + jnp.where(has_high, 1, 0) + extra)
 
     counter = iter(range(64))
 
@@ -174,10 +189,26 @@
             src_ref=src, dst_ref=dst, send_sem=send_sem.at[i], recv_sem=recv_sem.at[i], device_id=device, device_id_type=MESH
         )
 
+    def again(i, src, dst, device):
+        return pltpu.make_async_remote_copy(
+            src_ref=src, dst_ref=dst, send_sem=send_sem.at[i], recv_sem=recv_sem.at[i], device_id=device, device_id_type=MESH
+        )
+
     three = pl.ds(0, 3)
-    tile = (slice(None), slice(None), slice(None), OWN_Z, OWN_X)
-    up = remote(pert.at[pl.ds(2, 2), :, three], low.at[tile], (jnp.minimum(h + 1, 7), gx, gz))
-    down = remote(pert.at[pl.ds(0, 2), :, three], high.at[tile], (jnp.maximum(h - 1, 0), gx, gz))
+
+    def tile(j):
+        return (pl.ds(j, 1), slice(None), slice(None), OWN_Z, OWN_X)
+
+    turn_up, turn_down = bent & (h == 3), bent & (h == 4)
+    pass_up, pass_down = bent & (h == 7), bent & (h == 0)
+    up, down, leg_up, leg_down, on_up, on_down = [], [], [], [], [], []
+    for j in range(2):
+        up.append(remote(pert.at[pl.ds(2 + j, 1), :, three], low.at[tile(j)], (jnp.minimum(h + 1, 7), gx, gz)))
+        down.append(remote(pert.at[pl.ds(j, 1), :, three], high.at[tile(j)], (jnp.maximum(h - 1, 0), gx, gz)))
+        leg_up.append(remote(pert.at[pl.ds(2 + j, 1), :, three], high.at[tile(j)], (7, gx, across)))
+        leg_down.append(remote(pert.at[pl.ds(j, 1), :, three], low.at[tile(j)], (0, gx, across)))
+        on_up.append(again(4 * j, high.at[tile(j)], low.at[tile(j)], (4, gx, across)))
+        on_down.append(again(4 * j + 1, low.at[tile(j)], high.at[tile(j)], (3, gx, across)))
     rim_x, rim_z, base_x, base_z = [], [], [], []
     for s in (1, -1):
         rim_z.append(remote(pert.at[:, :, :, BARE_Z[s]], own.at[:, :, :, RIM_Z[s], OWN_X], (h, gx, side_z[s])))
@@ -187,27 +218,65 @@
             fields = pl.ds(at, 3)
             base_x.append(remote(ref.at[:, :, BARE_X[s]], flow.at[fields, OWN_Z, RIM_X[s]], (h, side_x[s], gz)))
             base_z.append(remote(ref.at[:, BARE_Z[s]], flow.at[fields, RIM_Z[s], OWN_X], (twin[s], gx, side_z[s])))
-    pl.when(has_high)(up.start)
-    pl.when(has_low)(down.start)
+    def starts(copies):
+        def run():
+            for copy in copies:
+                copy.start()
+
+        return run
+
+    def arrivals(copies):
+        def run():
+            for copy in copies:
+                copy.wait_recv()
+
+        return run
+
+    def departures(copies):
+        def run():
+            for copy in copies:
+                copy.wait_send()
+
+        return run
+
+    up_here, down_here = has_high & jnp.logical_not(turn_up), has_low & jnp.logical_not(turn_down)
+    pl.when(up_here)(starts(up))
+    pl.when(turn_up)(starts(leg_up))
+    pl.when(down_here)(starts(down))
+    pl.when(turn_down)(starts(leg_down))
     for copy in rim_x + rim_z + base_x + base_z:
         copy.start()
-    corner = {}
+
+    near_x = {}
     for name, ref in (("low", low), ("high", high)):
-        corner[name, "x"] = [
+        near_x[name] = [
             remote(ref.at[:, :, :, OWN_Z, SLAB_X[s]], ref.at[:, :, :, OWN_Z, RIM_X[s]], (h, side_x[s], gz)) for s in (1, -1)
         ]
-        corner[name, "z"] = [
-            remote(ref.at[:, :, :, SLAB_Z[s], OWN_X], ref.at[:, :, :, RIM_Z[s], OWN_X], (h, gx, side_z[s])) for s in (1, -1)
+
+    def beside(ref):
+        return [remote(ref.at[:, :, :, SLAB_Z[s], OWN_X], ref.at[:, :, :, RIM_Z[s], OWN_X], (h, gx, side_z[s])) for s in (1, -1)]
+
+    def onward(harmonics, ref, target):
+        return [
+            remote(own.at[harmonics, :, three, RIM_Z[s], OWN_X], ref.at[:, :, :, RIM_Z[s], OWN_X], (target, gx, gz)) for s in (1, -1)
         ]
 
-    def stage(ref, shape, first, layers, rows):
+    lower = h < 4
+    upper = jnp.logical_not(lower)
+    high_x, low_x = beside(high), beside(low)
+    low_y = onward(pl.ds(2, 2), low, jnp.minimum(h + 1, 7))
+    high_y = onward(pl.ds(0, 2), high, jnp.maximum(h - 1, 0))
+    corners = [(high_x, lower, lower), (low_x, upper, upper), (low_y, h < 3, lower & has_low), (high_y, h > 4, upper & has_high)]
+
+    def stage(ref, shape, first, layers, rows, scale=None):
         def body(i, carry):
             index, rest = [], i
             for size in reversed(shape):
                 index.insert(0, lax.rem(rest, size))
                 rest = lax.div(rest, size)
             for z in layers:
-                slabs[first + i, z, rows, :] = ref[(*index, z, rows)].astype(jnp.float32)
+                value = ref[(*index, z, rows)].astype(jnp.float32)
+                slabs[first + i, z, rows, :] = value if scale is None else value * scale
             return carry
 
         count = 1
@@ -222,7 +291,7 @@
     for copy in rim_x + base_x:
         copy.wait_recv()
     stage(own, (4, 2, 4), OWN0, middle, every)
-    stage(flow, (15,), BASE0, middle, every)
+    stage(flow, (15,), BASE0, middle, every, TWELFTH)
 
     lanes = lax.broadcasted_iota(jnp.int32, (8, LANES), 1)
     masks = {1: lanes < LANES - 1, 2: lanes < LANES - 2, -1: lanes >= 1, -2: lanes >= 2}
@@ -241,30 +310,40 @@
 
         lax.fori_loop(0, 6, layer, 0)
 
-    sweep([(OWN, (0, 1))], True)
-
-    def relay(present, ref, name, arrival, first):
-        @pl.when(present)
-        def _():
-            arrival.wait_recv()
-            for copy in corner[name, "z"] + corner[name, "x"]:
-                copy.start()
-
-    relay(has_low, low, "low", up, LOW0)
-    relay(has_high, high, "high", down, HIGH0)
+    def pass_on(z):
+        for j in range(2):
+            for present, leg, second in ((pass_up, leg_up, on_up), (pass_down, leg_down, on_down)):
+
+                @pl.when(present & (z == 2 + 2 * j))
+                def _(leg=leg[j], second=second[j]):
+                    leg.wait_recv()
+                    second.start()
+
+    sweep([(OWN, (0, 1))], True, pass_on)
     for copy in rim_z + base_z:
         copy.wait_recv()
+    pl.when(h < 3)(starts(low_y))
+    pl.when(h > 4)(starts(high_y))
     stage(own, (4, 2, 4), OWN0, edge, OWN_X)
-    stage(flow, (15,), BASE0, edge, OWN_X)
-    sweep([(OWN, (2,))], False)
+    stage(flow, (15,), BASE0, edge, OWN_X, TWELFTH)
+
+    def spread(z):
+        for present, copies, name, half, beside_z in ((has_low, up, "low", upper, low_x), (has_high, down, "high", lower, high_x)):
+
+            @pl.when(present & (z == 2))
+            def _(copies=copies, name=name):
+                arrivals(copies)()
+                starts(near_x[name])()
+
+            pl.when(half & (z == 2))(starts(beside_z))
+
+    sweep([(OWN, (2,))], False, spread)
 
     def settle(present, ref, name, first):
         @pl.when(present)
         def _():
-            for copy in corner[name, "z"] + corner[name, "x"]:
-                copy.wait_recv()
+            arrivals(near_x[name])()
             stage(ref, (2, 2, 3), first, middle, every)
-            stage(ref, (2, 2, 3), first, edge, OWN_X)
 
         @pl.when(jnp.logical_not(present))
         def _():
@@ -276,11 +355,19 @@
 
     settle(has_low, low, "low", LOW0)
     settle(has_high, high, "high", HIGH0)
+    sweep([(OTHERS, (0, 1))], False)
+    for copies, _, comes in corners:
+        pl.when(comes)(arrivals(copies))
+    for present, ref, first in ((has_low, low, LOW0), (has_high, high, HIGH0)):
+
+        @pl.when(present)
+        def _(ref=ref, first=first):
+            stage(ref, (2, 2, 3), first, edge, OWN_X)
 
     def write(z):
         return pltpu.make_async_copy(out.at[:, :, :, z], out_hbm.at[:, :, :, z], out_sem.at[z])
 
-    sweep([(OTHERS, (0, 1, 2))], False, lambda z: write(z).start())
+    sweep([(OTHERS, (2,))], False, lambda z: write(z).start())
 
     def drain(z, carry):
         write(z).wait()
@@ -289,14 +376,16 @@
     lax.fori_loop(0, 6, drain, 0)
     for copy in rim_x + rim_z + base_x + base_z:
         copy.wait_send()
-    pl.when(has_high)(up.wait_send)
-    pl.when(has_low)(down.wait_send)
-    for present, name in ((has_low, "low"), (has_high, "high")):
-
-        @pl.when(present)
-        def _(name=name):
-            for copy in corner[name, "z"] + corner[name, "x"]:
-                copy.wait_send()
+    pl.when(up_here)(departures(up))
+    pl.when(turn_up)(departures(leg_up))
+    pl.when(pass_up)(departures(on_up))
+    pl.when(down_here)(departures(down))
+    pl.when(turn_down)(departures(leg_down))
+    pl.when(pass_down)(departures(on_down))
+    pl.when(has_low)(departures(near_x["low"]))
+    pl.when(has_high)(departures(near_x["high"]))
+    for copies, goes, _ in corners:
+        pl.when(goes)(departures(copies))
 
 
 def shards(perturbation, base_mean, base_modes, solid_mask):
@@ -320,8 +409,8 @@
             pltpu.VMEM(turned.shape, jnp.float32),
             pltpu.VMEM(mask.shape, jnp.int32),
             pltpu.SemaphoreType.DMA((7,)),
-            pltpu.SemaphoreType.DMA((34,)),
-            pltpu.SemaphoreType.DMA((34,)),
+            pltpu.SemaphoreType.DMA((44,)),
+            pltpu.SemaphoreType.DMA((44,)),
             pltpu.SemaphoreType.DMA((6,)),
         ],
         compiler_params=pltpu.CompilerParams(collective_id=0, has_side_effects=True, vmem_limit_bytes=60 * 1024 * 1024),

time: 51.7 us -> 47.5 us (0.919)
  the two profiles are of different devices: /device:TPU:25 before, /device:TPU:0 now
where the time goes in v2:
time: 47.5 us; the launch traced here: 47.4 us
  Pallas kernels  43.3 us (91%)
  local copies, waits for them, and re-layouts  4.05 us (9%)
    pallas_call x1, Pallas kernels, shards(): pl.pallas_call(kernel, out_shape=jax.ShapeDtypeStruct(turned.shape, jnp.f...  43.3 us
    unnamed x1, local copies, waits for them, and re-layouts  4.05 us

profile of v2, /device:TPU:0, one launch (start us, length us, event | category | flops | bytes accessed | tf_op | source)
XLA Modules:
  0.0 47.4 jit_solution(3375200891315755963)
XLA Ops:
  0.0 43.3 %shard_map.46 = f32[4,2,4,6,32,128]{5,4,3,2,1,0:T(8,128)} custom-call(bf16[4,2,4,6,32,128]{5,4,3,2,1,0:T(8,128)(2,1)} %bitcast.6, bf16[3,6,32,128]{3,2,1,0:T(8,128)(2,1)} %bitcast.8, bf16[2,2,3,6,32,128]{5,4,3,2,1,0:T(8,128)(2,1)} %bitcast.7, s32[6,32,128]{2,1,0:T(8,128)} %bitcast.9), custom_call_target="tpu_custom_call" | custom-call | tf_op jit(solution)/shard_map/pallas_call | solution.py:398
  43.3 4.0 %copy.6 = f32[4,2,4,32,6,128]{5,3,4,2,1,0:T(8,128)} copy(f32[4,2,4,32,6,128]{5,3,4,2,1,0:T(8,128)} %bitcast.5) | data formatting | bytes 6291456

commit v3 on v1

--- a/solution.py
+++ b/solution.py
@@ -12,14 +12,11 @@
 MESH = pl.DeviceIdType.MESH
 
 LAYERS, ROWS, LANES = 10, 48, 128
+SEMAPHORES = 48
 OWN_Z = pl.ds(2, 6)
 OWN_X = pl.ds(8, 32)
-RIM_Z = {1: pl.ds(0, 2), -1: pl.ds(8, 2)}
 RIM_X = {1: pl.ds(6, 2), -1: pl.ds(40, 2)}
-BARE_Z = {1: pl.ds(4, 2), -1: pl.ds(0, 2)}
 BARE_X = {1: pl.ds(30, 2), -1: pl.ds(0, 2)}
-SLAB_Z = {1: pl.ds(6, 2), -1: pl.ds(2, 2)}
-SLAB_X = {1: pl.ds(38, 2), -1: pl.ds(8, 2)}
 
 OWN0, LOW0, HIGH0, BASE0, FIELDS = 0, 32, 44, 56, 71
 
@@ -63,11 +60,11 @@
         return 8.0 * (s[0] - s[1]) - (s[2] - s[3])
 
     used = sorted({d for _, dirs in jobs for d in dirs})
-    flow = {(m, part, d): load(base(m, part, d)) * TWELFTH for m, part in MODES for d in used}
+    flow = {(m, part, d): load(base(m, part, d)) for m, part in MODES for d in used}
     solid = PENALTY * mask[z, here, :].astype(jnp.float32) if first else None
     diverge = {}
     for c in range(3):
-        bend = {(m, part, d): slope(sides(base(m, part, c), d)) * TWELFTH for m, part in MODES for d in used}
+        bend = {(m, part, d): slope(sides(base(m, part, c), d)) for m, part in MODES for d in used}
         total = {}
         if not first:
             total = {(k, part): out[k, part, c, z, here, :] for k in OWN for part in range(2)}
@@ -123,12 +120,11 @@
         out[k, part, 3, z, here, :] = value if first else out[k, part, 3, z, here, :] + value
 
 
-def kernel(pert, mean, modes, solid_hbm, out_hbm, own, low, high, flow, slabs, out, solid, local_sem, send_sem, recv_sem, out_sem):
+def kernel(pert, mean, modes, solid_hbm, out, own, low, high, flow, slabs, passing, solid, local_sem, send_sem, recv_sem):
     h, gx, gz = lax.axis_index("harm"), lax.axis_index("gx"), lax.axis_index("gz")
     side_x = {1: lax.rem(gx + 1, 4), -1: lax.rem(gx + 3, 4)}
     side_z = {1: lax.rem(gz + 1, 4), -1: lax.rem(gz + 3, 4)}
     odd = lax.rem(gz, 2)
-    twin = {1: lax.rem(h + 4 * odd, 8), -1: lax.rem(h + 4 * (1 - odd), 8)}
     has_low, has_high = h > 0, h < 7
 
     barrier = pltpu.get_barrier_semaphore()
@@ -140,6 +136,20 @@
         greet((h, side_x[s], gz))
         greet((h, gx, side_z[s]))
     greet((lax.rem(h + 4, 8), gx, 3 - gz))
+
+    inner = jnp.logical_or(h == 3, h == 4)
+    outer = jnp.logical_or(h == 0, h == 7)
+
+    @pl.when(inner)
+    def _():
+        greet((7 - h, gx, 3 - gz))
+
+    fellow = jnp.where(inner, 7 * lax.div(h, 4), 3 + lax.div(h, 4))
+
+    @pl.when(jnp.logical_or(inner, outer))
+    def _():
+        greet((fellow, gx, gz))
+        greet((fellow, gx, 3 - gz))
 
     @pl.when(has_low)
     def _():
@@ -164,50 +174,117 @@
     for copy in loads:
         copy.start()
 
-    pl.semaphore_wait(barrier, 5 + jnp.where(has_low, 1, 0) + jnp.where(has_high, 1, 0))
-
-    counter = iter(range(64))
+    extra = jnp.where(jnp.logical_or(inner, outer), 2, 0) + jnp.where(inner, 1, 0)
+    pl.semaphore_wait(barrier, 5 + jnp.where(has_low, 1, 0) + jnp.where(has_high, 1, 0) + extra)
+
+    counter, places = iter(range(SEMAPHORES)), {}
 
     def remote(src, dst, device):
         i = next(counter)
-        return pltpu.make_async_remote_copy(
+        copy = pltpu.make_async_remote_copy(
             src_ref=src, dst_ref=dst, send_sem=send_sem.at[i], recv_sem=recv_sem.at[i], device_id=device, device_id_type=MESH
         )
+        places[id(copy)] = i
+        return copy
+
+    def onto(first, src, dst, device):
+        return pltpu.make_async_remote_copy(
+            src_ref=src,
+            dst_ref=dst,
+            send_sem=send_sem.at[next(counter)],
+            recv_sem=recv_sem.at[places[id(first)]],
+            device_id=device,
+            device_id_type=MESH,
+        )
 
     three = pl.ds(0, 3)
-    tile = (slice(None), slice(None), slice(None), OWN_Z, OWN_X)
-    up = remote(pert.at[pl.ds(2, 2), :, three], low.at[tile], (jnp.minimum(h + 1, 7), gx, gz))
-    down = remote(pert.at[pl.ds(0, 2), :, three], high.at[tile], (jnp.maximum(h - 1, 0), gx, gz))
-    rim_x, rim_z, base_x, base_z = [], [], [], []
+
+    up = remote(pert.at[pl.ds(2, 2), :, three], low.at[:, :, :, OWN_Z, OWN_X], (jnp.minimum(h + 1, 7), gx, gz))
+    down = remote(pert.at[pl.ds(0, 2), :, three], high.at[:, :, :, OWN_Z, OWN_X], (jnp.maximum(h - 1, 0), gx, gz))
+    rim_x, base_x, base_mate, base_off = [], [], [], []
     for s in (1, -1):
-        rim_z.append(remote(pert.at[:, :, :, BARE_Z[s]], own.at[:, :, :, RIM_Z[s], OWN_X], (h, gx, side_z[s])))
         rim_x.append(remote(pert.at[:, :, :, :, BARE_X[s]], own.at[:, :, :, OWN_Z, RIM_X[s]], (h, side_x[s], gz)))
         pieces = [(mean, 0)] + [(modes.at[m, part], 3 + (m * 2 + part) * 3) for m in range(2) for part in range(2)]
         for ref, at in pieces:
             fields = pl.ds(at, 3)
             base_x.append(remote(ref.at[:, :, BARE_X[s]], flow.at[fields, OWN_Z, RIM_X[s]], (h, side_x[s], gz)))
-            base_z.append(remote(ref.at[:, BARE_Z[s]], flow.at[fields, RIM_Z[s], OWN_X], (twin[s], gx, side_z[s])))
+    off, far_off = 8 * odd, 8 * (1 - odd)
+    mate = gz + 1 - 2 * odd
+    to_mate, to_off = pl.ds(4 * (1 - odd), 2), pl.ds(4 * odd, 2)
+    at_mate, at_off = pl.ds(8 * odd, 2), pl.ds(far_off, 2)
+    rim_mate = remote(pert.at[:, :, :, to_mate], own.at[:, :, :, at_mate, OWN_X], (h, gx, mate))
+    rim_off = [
+        remote(pert.at[half, :, :, to_off], own.at[half, :, :, at_off, OWN_X], (h, gx, 3 - gz)) for half in (pl.ds(0, 2), pl.ds(2, 2))
+    ]
+    detour = remote(pert.at[pl.ds(2, 2), :, :, to_off], passing, (fellow, gx, gz))
+    resume = onto(rim_off[1], passing, own.at[pl.ds(2, 2), :, :, at_off, OWN_X], (fellow, gx, 3 - gz))
+    for ref, at in pieces:
+        fields = pl.ds(at, 3)
+        base_mate.append(remote(ref.at[:, to_mate], flow.at[fields, at_mate, OWN_X], (h, gx, mate)))
+        base_off.append(remote(ref.at[:, to_off], flow.at[fields, at_off, OWN_X], (lax.rem(h + 4, 8), gx, 3 - gz)))
+
+    def starts(copies):
+        def run():
+            for copy in copies:
+                copy.start()
+
+        return run
+
+    def arrivals(copies):
+        def run():
+            for copy in copies:
+                copy.wait_recv()
+
+        return run
+
+    def departures(copies):
+        def run():
+            for copy in copies:
+                copy.wait_send()
+
+        return run
+
     pl.when(has_high)(up.start)
     pl.when(has_low)(down.start)
-    for copy in rim_x + rim_z + base_x + base_z:
+    pl.when(inner)(detour.start)
+    for copy in [*rim_x, *base_x, rim_mate, *base_mate]:
         copy.start()
-    corner = {}
-    for name, ref in (("low", low), ("high", high)):
-        corner[name, "x"] = [
-            remote(ref.at[:, :, :, OWN_Z, SLAB_X[s]], ref.at[:, :, :, OWN_Z, RIM_X[s]], (h, side_x[s], gz)) for s in (1, -1)
+
+    @pl.when(jnp.logical_not(inner))
+    def _():
+        starts(rim_off)()
+        starts(base_off)()
+
+    forward_x, forward_z, straight_z, beside_z, across_z = {}, {}, {}, {}, {}
+    for name, ref, side in (("low", low, 1), ("high", high, -1)):
+        harmonics = pl.ds(2, 2) if side == 1 else pl.ds(0, 2)
+        target = jnp.clip(h + side, 0, 7)
+        forward_x[name] = [
+            remote(own.at[harmonics, :, three, OWN_Z, RIM_X[s]], ref.at[:, :, :, OWN_Z, RIM_X[s]], (target, gx, gz)) for s in (1, -1)
         ]
-        corner[name, "z"] = [
-            remote(ref.at[:, :, :, SLAB_Z[s], OWN_X], ref.at[:, :, :, RIM_Z[s], OWN_X], (h, gx, side_z[s])) for s in (1, -1)
-        ]
-
-    def stage(ref, shape, first, layers, rows):
+        rim = pl.ds(off, 2)
+        forward_z[name] = remote(own.at[harmonics, :, three, rim, OWN_X], ref.at[:, :, :, rim, OWN_X], (target, gx, gz))
+        straight_z[name] = onto(
+            forward_z[name], pert.at[harmonics, :, three, to_off], ref.at[:, :, :, at_off, OWN_X], (target, gx, 3 - gz)
+        )
+        across_z[name] = onto(
+            forward_z[name], ref.at[:, :, :, pl.ds(2 + 4 * odd, 2), OWN_X], ref.at[:, :, :, at_off, OWN_X], (h, gx, 3 - gz)
+        )
+        beside_z[name] = remote(
+            ref.at[:, :, :, pl.ds(6 - 4 * odd, 2), OWN_X], ref.at[:, :, :, at_mate, OWN_X], (h, gx, mate)
+        )
+    cross_up, cross_down = h == 3, h == 4
+    onward_up, onward_down = has_high & jnp.logical_not(inner), has_low & jnp.logical_not(inner)
+
+    def stage(ref, shape, first, layers, rows, scale=None):
         def body(i, carry):
             index, rest = [], i
             for size in reversed(shape):
                 index.insert(0, lax.rem(rest, size))
                 rest = lax.div(rest, size)
             for z in layers:
-                slabs[first + i, z, rows, :] = ref[(*index, z, rows)].astype(jnp.float32)
+                value = ref[(*index, z, rows)].astype(jnp.float32)
+                slabs[first + i, z, rows, :] = value if scale is None else value * scale
             return carry
 
         count = 1
@@ -219,10 +296,14 @@
     every = pl.ds(0, ROWS)
     for copy in loads:
         copy.wait()
-    for copy in rim_x + base_x:
+    for copy in rim_x:
         copy.wait_recv()
+    pl.when(has_high)(starts(forward_x["low"]))
+    pl.when(has_low)(starts(forward_x["high"]))
+    pl.when(inner)(rim_off[0].start)
+    arrivals(base_x)()
     stage(own, (4, 2, 4), OWN0, middle, every)
-    stage(flow, (15,), BASE0, middle, every)
+    stage(flow, (15,), BASE0, middle, every, TWELFTH)
 
     lanes = lax.broadcasted_iota(jnp.int32, (8, LANES), 1)
     masks = {1: lanes < LANES - 1, 2: lanes < LANES - 2, -1: lanes >= 1, -2: lanes >= 2}
@@ -241,30 +322,40 @@
 
         lax.fori_loop(0, 6, layer, 0)
 
-    sweep([(OWN, (0, 1))], True)
-
-    def relay(present, ref, name, arrival, first):
-        @pl.when(present)
+    def pass_on(z):
+        @pl.when(outer & (z == 4))
         def _():
-            arrival.wait_recv()
-            for copy in corner[name, "z"] + corner[name, "x"]:
-                copy.start()
-
-    relay(has_low, low, "low", up, LOW0)
-    relay(has_high, high, "high", down, HIGH0)
-    for copy in rim_z + base_z:
-        copy.wait_recv()
-    stage(own, (4, 2, 4), OWN0, edge, OWN_X)
-    stage(flow, (15,), BASE0, edge, OWN_X)
-    sweep([(OWN, (2,))], False)
+            detour.wait_recv()
+            resume.start()
+
+    sweep([(OWN, (0, 1))], True, pass_on)
+
+    @pl.when(inner)
+    def _():
+        starts(base_off)()
+        pl.when(cross_up)(straight_z["low"].start)
+        pl.when(cross_down)(straight_z["high"].start)
+
+    def own_rims():
+        arrivals([rim_mate, *rim_off])()
+        pl.when(onward_up)(forward_z["low"].start)
+        pl.when(onward_down)(forward_z["high"].start)
+
+    def neighbours():
+        for present, copy, name, there in ((has_low, up, "low", h == 5), (has_high, down, "high", h == 2)):
+
+            @pl.when(present)
+            def _(copy=copy, name=name):
+                copy.wait_recv()
+                beside_z[name].start()
+
+            pl.when(there)(across_z[name].start)
 
     def settle(present, ref, name, first):
         @pl.when(present)
         def _():
-            for copy in corner[name, "z"] + corner[name, "x"]:
-                copy.wait_recv()
+            arrivals(forward_x[name])()
             stage(ref, (2, 2, 3), first, middle, every)
-            stage(ref, (2, 2, 3), first, edge, OWN_X)
 
         @pl.when(jnp.logical_not(present))
         def _():
@@ -274,29 +365,53 @@
 
             lax.fori_loop(0, 12, clear, 0)
 
-    settle(has_low, low, "low", LOW0)
-    settle(has_high, high, "high", HIGH0)
-
-    def write(z):
-        return pltpu.make_async_copy(out.at[:, :, :, z], out_hbm.at[:, :, :, z], out_sem.at[z])
-
-    sweep([(OTHERS, (0, 1, 2))], False, lambda z: write(z).start())
-
-    def drain(z, carry):
-        write(z).wait()
-        return carry
-
-    lax.fori_loop(0, 6, drain, 0)
-    for copy in rim_x + rim_z + base_x + base_z:
-        copy.wait_send()
+    def others():
+        settle(has_low, low, "low", LOW0)
+        settle(has_high, high, "high", HIGH0)
+        sweep([(OTHERS, (0, 1))], False)
+
+    late = jnp.logical_or(inner, outer)
+    pl.when(jnp.logical_not(inner))(own_rims)
+
+    @pl.when(late)
+    def _():
+        neighbours()
+        others()
+
+    pl.when(inner)(own_rims)
+    arrivals(base_mate + base_off)()
+    stage(own, (4, 2, 4), OWN0, edge, OWN_X)
+    stage(flow, (15,), BASE0, edge, OWN_X, TWELFTH)
+
+    def spread(z):
+        pl.when(jnp.logical_not(late) & (z == 2))(neighbours)
+
+    sweep([(OWN, (2,))], False, spread)
+    pl.when(jnp.logical_not(late))(others)
+    for present, ref, name, first in ((has_low, low, "low", LOW0), (has_high, high, "high", HIGH0)):
+
+        @pl.when(present)
+        def _(ref=ref, name=name, first=first):
+            forward_z[name].wait_recv()
+            beside_z[name].wait_recv()
+            stage(ref, (2, 2, 3), first, edge, OWN_X)
+
+    sweep([(OTHERS, (2,))], False)
+    departures([*rim_x, *base_x, rim_mate, rim_off[0], *base_mate, *base_off])()
+    pl.when(jnp.logical_not(inner))(rim_off[1].wait_send)
+    pl.when(inner)(detour.wait_send)
+    pl.when(outer)(resume.wait_send)
     pl.when(has_high)(up.wait_send)
     pl.when(has_low)(down.wait_send)
+    for goes, onward, name in ((has_high, onward_up, "low"), (has_low, onward_down, "high")):
+        pl.when(goes)(departures(forward_x[name]))
+        pl.when(onward)(forward_z[name].wait_send)
+    pl.when(cross_up)(straight_z["low"].wait_send)
+    pl.when(cross_down)(straight_z["high"].wait_send)
+    pl.when(h == 5)(across_z["low"].wait_send)
+    pl.when(h == 2)(across_z["high"].wait_send)
     for present, name in ((has_low, "low"), (has_high, "high")):
-
-        @pl.when(present)
-        def _(name=name):
-            for copy in corner[name, "z"] + corner[name, "x"]:
-                copy.wait_send()
+        pl.when(present)(beside_z[name].wait_send)
 
 
 def shards(perturbation, base_mean, base_modes, solid_mask):
@@ -305,27 +420,27 @@
     modes = jnp.transpose(base_modes, (0, 1, 2, 4, 3, 5))
     mask = jnp.transpose(solid_mask, (1, 0, 2))
     anywhere = pl.BlockSpec(memory_space=pl.ANY)
+    vmem = pl.BlockSpec(memory_space=pltpu.VMEM)
     half = jnp.bfloat16
     out = pl.pallas_call(
         kernel,
         out_shape=jax.ShapeDtypeStruct(turned.shape, jnp.float32),
         in_specs=[anywhere] * 4,
-        out_specs=anywhere,
+        out_specs=vmem,
         scratch_shapes=[
             pltpu.VMEM((4, 2, 4, LAYERS, ROWS, LANES), half),
             pltpu.VMEM((2, 2, 3, LAYERS, ROWS, LANES), half),
             pltpu.VMEM((2, 2, 3, LAYERS, ROWS, LANES), half),
             pltpu.VMEM((15, LAYERS, ROWS, LANES), half),
             pltpu.VMEM((FIELDS, LAYERS, ROWS, LANES), jnp.float32),
-            pltpu.VMEM(turned.shape, jnp.float32),
+            pltpu.VMEM((2, 2, 4, 2, 32, LANES), half),
             pltpu.VMEM(mask.shape, jnp.int32),
             pltpu.SemaphoreType.DMA((7,)),
-            pltpu.SemaphoreType.DMA((34,)),
-            pltpu.SemaphoreType.DMA((34,)),
-            pltpu.SemaphoreType.DMA((6,)),
+            pltpu.SemaphoreType.DMA((SEMAPHORES,)),
+            pltpu.SemaphoreType.DMA((SEMAPHORES,)),
         ],
-        compiler_params=pltpu.CompilerParams(collective_id=0, has_side_effects=True, vmem_limit_bytes=60 * 1024 * 1024),
-    )(turned, mean, modes, mask)
+        compiler_params=pltpu.CompilerParams(collective_id=0, has_side_effects=True, vmem_limit_bytes=36 * 1024 * 1024),
+    )(*(pltpu.with_memory_space_constraint(array, pltpu.MemorySpace.HBM) for array in (turned, mean, modes, mask)))
     return jnp.transpose(out, (0, 1, 2, 4, 3, 5))
 
 

time: 51.7 us -> 39.8 us (0.77)
  the two profiles are of different devices: /device:TPU:25 before, /device:TPU:120 now
where the time goes in v3:
time: 39.8 us; the launch traced here: 39.7 us
  Pallas kernels  38 us (95%)
  local copies, waits for them, and re-layouts  1.67 us (4%)
    pallas_call x1, Pallas kernels, shards(): pl.pallas_call(kernel, out_shape=jax.ShapeDtypeStruct(turned.shape, jnp.f...  38 us
    unnamed x1, local copies, waits for them, and re-layouts  1.67 us

profile of v3, /device:TPU:120, one launch (start us, length us, event | category | flops | bytes accessed | tf_op | source)
XLA Modules:
  0.0 39.7 jit_solution(15877707563381515095)
XLA Ops:
  0.0 38.0 %shard_map.46 = f32[4,2,4,6,32,128]{5,4,3,2,1,0:T(8,128)S(1)} custom-call(bf16[4,2,4,6,32,128]{5,4,3,2,1,0:T(8,128)(2,1)} %bitcast.6, bf16[3,6,32,128]{3,2,1,0:T(8,128)(2,1)} %bitcast.8, bf16[2,2,3,6,32,128]{5,4,3,2,1,0:T(8,128)(2,1)} %bitcast.7, s32[6,32,128]{2,1,0:T(8,128)} %bitcast.9), custom_call_target="tpu_custom_call" | custom-call | tf_op jit(solution)/shard_map/pallas_call | solution.py:425
  38.0 1.7 %copy.6 = f32[4,2,4,32,6,128]{5,3,4,2,1,0:T(8,128)} copy(f32[4,2,4,32,6,128]{5,3,4,2,1,0:T(8,128)S(1)} %bitcast.5) | data formatting | bytes 6291456

commit v4 on v3

v4 whole, which is shorter than its diff:
```python
import jax
import jax.numpy as jnp
from jax import lax
from jax.experimental import pallas as pl
from jax.experimental.pallas import tpu as pltpu
from jax.sharding import PartitionSpec as P

FREQUENCY_STEP = 0.2
VISCOSITY = 0.05
PENALTY = 4.0
TWELFTH = 1.0 / 12.0
MESH = pl.DeviceIdType.MESH

LAYERS, ROWS, LANES = 10, 48, 128
SEMAPHORES = 56
OWN_BASE = 2
OWN_Z = pl.ds(2, 6)
OWN_X = pl.ds(8, 32)
RIM_X = {1: pl.ds(6, 2), -1: pl.ds(40, 2)}
BARE_X = {1: pl.ds(30, 2), -1: pl.ds(0, 2)}

OWN0, LOW0, HIGH0, BASE0, FIELDS = 0, 32, 44, 56, 71


def vel(l, part, c):
    if l < 0:
        return LOW0 + ((l + 2) * 2 + part) * 3 + c
    if l > 3:
        return HIGH0 + ((l - 4) * 2 + part) * 3 + c
    return OWN0 + (l * 2 + part) * 4 + c


def base(m, part, c):
    return BASE0 + (c if m == 0 else 3 + ((m - 1) * 2 + part) * 3 + c)


MODES = [(0, 0), (1, 0), (1, 1), (2, 0), (2, 1)]
OWN = (0, 1, 2, 3)
OTHERS = (-2, -1, 4, 5)


def block(slabs, slopes, bends, mask, out, freqs, z, xb, jobs, first):
    row = xb * 8 + 8
    here = pl.ds(xb * 8, 8)

    def load(field, dz=0, dx=0):
        return slabs[field, z + 2 + dz, pl.ds(row + dx, 8), :]

    def sides(field, d):
        if d == 0:
            return tuple(load(field, 0, o) for o in (1, -1, 2, -2))
        return tuple(load(field, o, 0) for o in (1, -1, 2, -2))

    def slope(s):
        return 8.0 * (s[0] - s[1]) - (s[2] - s[3])

    def along(field, d):
        return slopes[field, z, here, :] if d == 1 else slope(sides(field, d))

    used = sorted({d for _, dirs in jobs for d in dirs})
    flow = {(m, part, d): load(base(m, part, d)) for m, part in MODES for d in used}
    solid = PENALTY * mask[z, here, :].astype(jnp.float32) if first else None
    diverge = {}
    for c in range(3):
        bend = {(m, part, d): along(base(m, part, c), d) for m, part in MODES for d in used}
        total = {}
        if not first:
            total = {(k, part): out[2 * k + part, c, z, here, :] for k in OWN for part in range(2)}

        def add(key, term):
            total[key] = total[key] + term if key in total else term

        def sub(key, term):
            total[key] = total[key] - term if key in total else -term

        for ls, dirs in jobs:
            for l in ls:
                grad = {}
                for part in range(2):
                    around = {d: sides(vel(l, part, c), d) for d in dirs if d != 1}
                    for d in dirs:
                        grad[part, d] = slopes[vel(l, part, c), z, here, :] if d == 1 else slope(around[d])
                    if l in OWN:
                        key = (l, part)
                        near = sum(side[0] + side[1] for side in around.values())
                        far = sum(side[2] + side[3] for side in around.values())
                        bent = 16.0 * near - far
                        if 1 in dirs:
                            bent = bent + bends[vel(l, part, c), z, here, :]
                        sub(key, (VISCOSITY * TWELFTH) * bent)
                        if 0 in dirs:
                            value = load(vel(l, part, c))
                            add(key, (solid + VISCOSITY * 60.0 * TWELFTH) * value)
                            turn = freqs[l] * load(vel(l, 1 - part, c))
                            (sub if part == 0 else add)(key, turn)
                        if c in dirs:
                            add(key, along(OWN0 + (l * 2 + part) * 4 + 3, c) * TWELFTH)
                            diverge[key] = diverge[key] + grad[part, c] if key in diverge else grad[part, c]
                speed = {(part, d): load(vel(l, part, d)) for part in range(2) for d in dirs}
                for k in OWN:
                    m = k - l
                    if abs(m) > 2:
                        continue
                    a = abs(m)
                    for d in dirs:
                        gr, gi = grad[0, d], grad[1, d]
                        ur, ui = speed[0, d], speed[1, d]
                        fr, br = flow[a, 0, d], bend[a, 0, d]
                        add((k, 0), fr * gr + ur * br)
                        add((k, 1), fr * gi + ui * br)
                        if a:
                            fi, bi = flow[a, 1, d], bend[a, 1, d]
                            real, imag = fi * gi + ui * bi, fi * gr + ur * bi
                            (sub if m > 0 else add)((k, 0), real)
                            (add if m > 0 else sub)((k, 1), imag)
        for key, value in total.items():
            out[2 * key[0] + key[1], c, z, here, :] = value
    for (k, part), value in diverge.items():
        value = value * TWELFTH
        out[2 * k + part, 3, z, here, :] = value if first else out[2 * k + part, 3, z, here, :] + value


def kernel(pert, mean, modes, solid_hbm, out, own, low, high, flow, slabs, slopes, bends, band, passing, solid, local_sem, send_sem, recv_sem):
    h, gx, gz = lax.axis_index("harm"), lax.axis_index("gx"), lax.axis_index("gz")
    side_x = {1: lax.rem(gx + 1, 4), -1: lax.rem(gx + 3, 4)}
    side_z = {1: lax.rem(gz + 1, 4), -1: lax.rem(gz + 3, 4)}
    odd = lax.rem(gz, 2)
    has_low, has_high = h > 0, h < 7

    barrier = pltpu.get_barrier_semaphore()

    def greet(device):
        pl.semaphore_signal(barrier, inc=1, device_id=device, device_id_type=MESH)

    for s in (1, -1):
        greet((h, side_x[s], gz))
        greet((h, gx, side_z[s]))
    greet((lax.rem(h + 4, 8), gx, 3 - gz))

    inner = jnp.logical_or(h == 3, h == 4)
    outer = jnp.logical_or(h == 0, h == 7)

    @pl.when(inner)
    def _():
        greet((7 - h, gx, 3 - gz))

    fellow = jnp.where(inner, 7 * lax.div(h, 4), 3 + lax.div(h, 4))

    @pl.when(jnp.logical_or(inner, outer))
    def _():
        greet((fellow, gx, gz))
        greet((fellow, gx, 3 - gz))

    @pl.when(has_low)
    def _():
        greet((h - 1, gx, gz))

    @pl.when(has_high)
    def _():
        greet((h + 1, gx, gz))

    def local(i, src, dst):
        return pltpu.make_async_copy(src, dst, local_sem.at[i])

    loads = [
        local(0, pert, own.at[:, :, OWN_Z, OWN_X]),
        local(1, mean, flow.at[pl.ds(0, 3), OWN_Z, OWN_X]),
        local(2, modes, flow.at[pl.ds(3, 12), OWN_Z, OWN_X]),
        local(3, solid_hbm, solid),
    ]
    for copy in loads:
        copy.start()

    extra = jnp.where(jnp.logical_or(inner, outer), 2, 0) + jnp.where(inner, 1, 0)
    pl.semaphore_wait(barrier, 5 + jnp.where(has_low, 1, 0) + jnp.where(has_high, 1, 0) + extra)

    counter, places = iter(range(SEMAPHORES)), {}

    def remote(src, dst, device):
        i = next(counter)
        copy = pltpu.make_async_remote_copy(
            src_ref=src, dst_ref=dst, send_sem=send_sem.at[i], recv_sem=recv_sem.at[i], device_id=device, device_id_type=MESH
        )
        places[id(copy)] = i
        return copy

    def onto(first, src, dst, device):
        return pltpu.make_async_remote_copy(
            src_ref=src,
            dst_ref=dst,
            send_sem=send_sem.at[next(counter)],
            recv_sem=recv_sem.at[places[id(first)]],
            device_id=device,
            device_id_type=MESH,
        )

    three = pl.ds(0, 3)

    up = remote(pert.at[pl.ds(4, 4), three], low.at[:, :, OWN_Z, OWN_X], (jnp.minimum(h + 1, 7), gx, gz))
    down = remote(pert.at[pl.ds(0, 4), three], high.at[:, :, OWN_Z, OWN_X], (jnp.maximum(h - 1, 0), gx, gz))
    rim_x, base_x, base_mate, base_off, base_own = [], [], [], [], []
    for s in (1, -1):
        rim_x.append(remote(pert.at[:, :, :, BARE_X[s]], own.at[:, :, OWN_Z, RIM_X[s]], (h, side_x[s], gz)))
        for ref, at, count in ((mean, 0, 3), (modes, 3, 12)):
            base_x.append(remote(ref.at[:, :, BARE_X[s]], flow.at[pl.ds(at, count), OWN_Z, RIM_X[s]], (h, side_x[s], gz)))

    off, far_off = 8 * odd, 8 * (1 - odd)
    mate = gz + 1 - 2 * odd
    to_mate, to_off = pl.ds(4 * (1 - odd), 2), pl.ds(4 * odd, 2)
    at_mate, at_off = pl.ds(8 * odd, 2), pl.ds(far_off, 2)
    rim_mate = remote(pert.at[:, :, to_mate], own.at[:, :, at_mate, OWN_X], (h, gx, mate))
    rim_off = [
        remote(pert.at[half, :, to_off], own.at[half, :, at_off, OWN_X], (h, gx, 3 - gz)) for half in (pl.ds(0, 4), pl.ds(4, 4))
    ]
    detour = remote(pert.at[pl.ds(4, 4), :, to_off], passing, (fellow, gx, gz))
    resume = onto(rim_off[1], passing, own.at[pl.ds(4, 4), :, at_off, OWN_X], (fellow, gx, 3 - gz))
    for ref, start, at, count in ((mean, 0, 0, 3), (modes, 0, 3, 6), (modes, 6, 9, 6)):
        source, fields = ref.at[pl.ds(start, count)], pl.ds(at, count)
        base_mate.append(remote(source.at[:, to_mate], flow.at[fields, at_mate, OWN_X], (h, gx, mate)))
        base_off.append(remote(source.at[:, to_off], flow.at[fields, at_off, OWN_X], (lax.rem(h + 4, 8), gx, 3 - gz)))
        if len(base_own) < OWN_BASE:
            base_own.append(onto(base_off[-1], source.at[:, to_off], flow.at[fields, at_off, OWN_X], (h, gx, 3 - gz)))

    def starts(copies):
        def run():
            for copy in copies:
                copy.start()

        return run

    def arrivals(copies):
        def run():
            for copy in copies:
                copy.wait_recv()

        return run

    def departures(copies):
        def run():
            for copy in copies:
                copy.wait_send()

        return run

    pl.when(has_high)(up.start)
    pl.when(has_low)(down.start)
    pl.when(inner)(detour.start)
    for copy in [*rim_x, *base_x, rim_mate, *base_mate]:
        copy.start()

    @pl.when(jnp.logical_not(inner))
    def _():
        starts(rim_off)()
        starts(base_off)()

    pl.when(inner)(starts(base_off[OWN_BASE:]))

    forward_x, forward_z, straight_z, beside_z, across_z = {}, {}, {}, {}, {}
    for name, ref, side in (("low", low, 1), ("high", high, -1)):
        harmonics = pl.ds(4, 4) if side == 1 else pl.ds(0, 4)
        target = jnp.clip(h + side, 0, 7)
        forward_x[name] = [
            remote(own.at[harmonics, three, OWN_Z, RIM_X[s]], ref.at[:, :, OWN_Z, RIM_X[s]], (target, gx, gz)) for s in (1, -1)
        ]
        rim = pl.ds(off, 2)
        forward_z[name] = remote(own.at[harmonics, three, rim, OWN_X], ref.at[:, :, rim, OWN_X], (target, gx, gz))
        straight_z[name] = onto(
            forward_z[name], pert.at[harmonics, three, to_off], ref.at[:, :, at_off, OWN_X], (target, gx, 3 - gz)
        )
        across_z[name] = onto(
            forward_z[name], ref.at[:, :, pl.ds(2 + 4 * odd, 2), OWN_X], ref.at[:, :, at_off, OWN_X], (h, gx, 3 - gz)
        )
        beside_z[name] = remote(
            ref.at[:, :, pl.ds(6 - 4 * odd, 2), OWN_X], ref.at[:, :, at_mate, OWN_X], (h, gx, mate)
        )
    cross_up, cross_down = h == 3, h == 4
    pl.when(cross_up)(straight_z["low"].start)
    pl.when(cross_down)(straight_z["high"].start)
    onward_up, onward_down = has_high & jnp.logical_not(inner), has_low & jnp.logical_not(inner)

    def stage(ref, first, layers, rows, scale=None):
        groups, width = ref.shape[:2]

        def body(i, carry):
            for c in range(width):
                for z in layers:
                    for part in rows:
                        value = ref[i, c, z, part].astype(jnp.float32)
                        slabs[first + i * width + c, z, part, :] = value if scale is None else value * scale
            return carry

        lax.fori_loop(0, groups, body, 0)

    def stage_own(ref, first, curved, scale=None):
        groups, width = ref.shape[:2]
        weights = band[...] if curved else band[:, pl.ds(0, LANES)]

        def body(i, carry):
            fields = pl.ds(first + i * width, width)
            tile = ref[i, :, OWN_Z, OWN_X]
            value = tile.astype(jnp.float32)
            slabs[fields, OWN_Z, OWN_X, :] = value if scale is None else value * scale
            product = jnp.dot(tile.reshape(width * 192, LANES), weights, preferred_element_type=jnp.float32)
            if scale is not None:
                product = product * scale
            slopes[fields] = product[:, :LANES].reshape(width, 6, 32, LANES)
            if curved:
                bends[fields] = product[:, LANES:].reshape(width, 6, 32, LANES)
            return carry

        lax.fori_loop(0, groups, body, 0)

    middle = range(2, 8)
    flow_groups = flow.reshape(5, 3, LAYERS, ROWS, LANES)
    x_rims = (pl.ds(0, 8), pl.ds(40, 8))
    shift = lax.broadcasted_iota(jnp.int32, (LANES, LANES), 0) - lax.broadcasted_iota(jnp.int32, (LANES, LANES), 1)
    first_band, second_band = jnp.zeros((LANES, LANES), jnp.float32), jnp.zeros((LANES, LANES), jnp.float32)
    for offset, one, two in ((1, 8.0, 16.0), (-1, -8.0, 16.0), (2, -1.0, -1.0), (-2, 1.0, -1.0), (0, 0.0, -30.0)):
        first_band = jnp.where(shift == offset, one, first_band)
        second_band = jnp.where(shift == offset, two, second_band)
    band[:, pl.ds(0, LANES)] = first_band.astype(band.dtype)
    band[:, pl.ds(LANES, LANES)] = second_band.astype(band.dtype)
    for copy in loads:
        copy.wait()
    stage_own(own, OWN0, True)
    stage_own(flow_groups, BASE0, False, TWELFTH)

    freqs = [FREQUENCY_STEP * (h * 4 + k - 16).astype(jnp.float32) for k in range(4)]

    def sweep(jobs, first=False, layers=(0, 6), chunks=(0, 1, 4), finish=None):
        start, step, count = chunks

        def layer(j, carry):
            z = layers[0] + j

            def chunk(i, inner_carry):
                block(slabs, slopes, bends, solid, out, freqs, z, start + step * i, jobs, first)
                return inner_carry

            lax.fori_loop(0, count, chunk, 0)
            if finish is not None:
                finish(j)
            return carry

        lax.fori_loop(0, layers[1], layer, 0)

    free, bound = (2 - 2 * odd, 4), (4 * odd, 2)
    mate_edge, off_edge = [far_off, far_off + 1], [off, off + 1]

    sweep([(OWN, (0, 1))], True, chunks=(1, 1, 2))
    arrivals(rim_x)()
    pl.when(has_high)(starts(forward_x["low"]))
    pl.when(has_low)(starts(forward_x["high"]))
    pl.when(inner)(rim_off[0].start)
    arrivals(base_x)()
    stage(own, OWN0, middle, x_rims)
    stage(flow_groups, BASE0, middle, x_rims, TWELFTH)

    def pass_on(j):
        @pl.when(outer & (j == 2))
        def _():
            detour.wait_recv()
            resume.start()
            starts(base_own)()

    sweep([(OWN, (0, 1))], True, chunks=(0, 3, 2), finish=pass_on)
    arrivals([rim_mate, *base_mate])()
    stage(own, OWN0, mate_edge, (OWN_X,))
    stage(flow_groups, BASE0, mate_edge, (OWN_X,), TWELFTH)
    sweep([(OWN, (2,))], layers=free)

    @pl.when(jnp.logical_not(inner))
    def _():
        arrivals(rim_off)()
        pl.when(onward_up)(forward_z["low"].start)
        pl.when(onward_down)(forward_z["high"].start)

    def neighbours():
        for present, copy, name, there in ((has_low, up, "low", h == 5), (has_high, down, "high", h == 2)):

            @pl.when(present)
            def _(copy=copy, name=name):
                copy.wait_recv()
                beside_z[name].start()

            pl.when(there)(across_z[name].start)

    neighbours()
    for present, ref, name, first in ((has_low, low, "low", LOW0), (has_high, high, "high", HIGH0)):

        @pl.when(present)
        def _(ref=ref, name=name, first=first):
            stage_own(ref, first, False)
            arrivals(forward_x[name])()
            stage(ref, first, middle, x_rims)
            beside_z[name].wait_recv()
            stage(ref, first, mate_edge, (OWN_X,))

        @pl.when(jnp.logical_not(present))
        def _(first=first):
            def clear(i, carry):
                slabs[first + i] = jnp.zeros((LAYERS, ROWS, LANES), jnp.float32)
                slopes[first + i] = jnp.zeros((6, 32, LANES), jnp.float32)
                return carry

            lax.fori_loop(0, 12, clear, 0)

    sweep([(OTHERS, (0, 1, 2))], layers=free)
    sweep([(OTHERS, (0, 1))], layers=bound)
    pl.when(inner)(arrivals(rim_off))
    arrivals(base_off)()
    stage(own, OWN0, off_edge, (OWN_X,))
    stage(flow_groups, BASE0, off_edge, (OWN_X,), TWELFTH)
    for present, ref, name, first in ((has_low, low, "low", LOW0), (has_high, high, "high", HIGH0)):

        @pl.when(present)
        def _(ref=ref, name=name, first=first):
            forward_z[name].wait_recv()
            stage(ref, first, off_edge, (OWN_X,))

    sweep([(OWN, (2,)), (OTHERS, (2,))], layers=bound)
    departures([*rim_x, *base_x, rim_mate, rim_off[0], *base_mate])()
    pl.when(jnp.logical_not(inner))(departures([rim_off[1], *base_off[:OWN_BASE]]))
    departures(base_off[OWN_BASE:])()
    pl.when(outer)(departures(base_own))
    pl.when(inner)(detour.wait_send)
    pl.when(outer)(resume.wait_send)
    pl.when(has_high)(up.wait_send)
    pl.when(has_low)(down.wait_send)
    for goes, onward, name in ((has_high, onward_up, "low"), (has_low, onward_down, "high")):
        pl.when(goes)(departures(forward_x[name]))
        pl.when(onward)(forward_z[name].wait_send)
    pl.when(cross_up)(straight_z["low"].wait_send)
    pl.when(cross_down)(straight_z["high"].wait_send)
    pl.when(h == 5)(across_z["low"].wait_send)
    pl.when(h == 2)(across_z["high"].wait_send)
    for present, name in ((has_low, "low"), (has_high, "high")):
        pl.when(present)(beside_z[name].wait_send)


def shards(perturbation, base_mean, base_modes, solid_mask):
    per, _, _, cx, cz, cy = perturbation.shape
    turned = jnp.transpose(perturbation, (0, 1, 2, 4, 3, 5)).reshape(per * 2, 4, cz, cx, cy)
    mean = jnp.transpose(base_mean, (0, 2, 1, 3))
    modes = jnp.transpose(base_modes, (0, 1, 2, 4, 3, 5)).reshape(12, cz, cx, cy)
    mask = jnp.transpose(solid_mask, (1, 0, 2))
    anywhere = pl.BlockSpec(memory_space=pl.ANY)
    vmem = pl.BlockSpec(memory_space=pltpu.VMEM)
    half = jnp.bfloat16
    out = pl.pallas_call(
        kernel,
        out_shape=jax.ShapeDtypeStruct(turned.shape, jnp.float32),
        in_specs=[anywhere] * 4,
        out_specs=vmem,
        scratch_shapes=[
            pltpu.VMEM((8, 4, LAYERS, ROWS, LANES), half),
            pltpu.VMEM((4, 3, LAYERS, ROWS, LANES), half),
            pltpu.VMEM((4, 3, LAYERS, ROWS, LANES), half),
            pltpu.VMEM((15, LAYERS, ROWS, LANES), half),
            pltpu.VMEM((FIELDS, LAYERS, ROWS, LANES), jnp.float32),
            pltpu.VMEM((FIELDS, 6, 32, LANES), jnp.float32),
            pltpu.VMEM((32, 6, 32, LANES), jnp.float32),
            pltpu.VMEM((LANES, 2 * LANES), half),
            pltpu.VMEM((4, 4, 2, 32, LANES), half),
            pltpu.VMEM(mask.shape, jnp.int32),
            pltpu.SemaphoreType.DMA((4,)),
            pltpu.SemaphoreType.DMA((SEMAPHORES,)),
            pltpu.SemaphoreType.DMA((SEMAPHORES,)),
        ],
        compiler_params=pltpu.CompilerParams(collective_id=0, has_side_effects=True, vmem_limit_bytes=46 * 1024 * 1024),
    )(*(pltpu.with_memory_space_constraint(array, pltpu.MemorySpace.HBM) for array in (turned, mean, modes, mask)))
    return jnp.transpose(out.reshape(per, 2, 4, cz, cx, cy), (0, 1, 2, 4, 3, 5))


def solution(mesh):
    return jax.shard_map(
        shards,
        mesh=mesh,
        in_specs=(
            P("harm", None, None, "gx", "gz", None),
            P(None, "gx", "gz", None),
            P(None, None, None, "gx", "gz", None),
            P("gx", "gz", None),
        ),
        out_specs=P("harm", None, None, "gx", "gz", None),
        check_vma=False,
    )
```

time: 39.8 us -> 37.3 us (0.937)
  the two profiles are of different devices: /device:TPU:120 before, /device:TPU:68 now
where the time goes in v4:
time: 37.3 us; the launch traced here: 37.2 us
  Pallas kernels  35.6 us (95%)
  local copies, waits for them, and re-layouts  1.67 us (4%)
    pallas_call x1, Pallas kernels, shards(): pl.pallas_call(kernel, out_shape=jax.ShapeDtypeStruct(turned.shape, jnp.f...  35.6 us
    unnamed x1, local copies, waits for them, and re-layouts  1.67 us

profile of v4, /device:TPU:68, one launch (start us, length us, event | category | flops | bytes accessed | tf_op | source)
XLA Modules:
  0.0 37.2 jit_solution(15532322336321422790)
XLA Ops:
  0.0 35.6 %shard_map.46 = f32[8,4,6,32,128]{4,3,2,1,0:T(8,128)S(1)} custom-call(bf16[8,4,6,32,128]{4,3,2,1,0:T(8,128)(2,1)} %bitcast.12, bf16[3,6,32,128]{3,2,1,0:T(8,128)(2,1)} %bitcast.14, bf16[12,6,32,128]{3,2,1,0:T(8,128)(2,1)} %bitcast.13, s32[6,32,128]{2,1,0:T(8,128)} %bitcast.15), custom_call_target="tpu_custom_call" | custom-call | tf_op jit(solution)/shard_map/pallas_call | solution.py:450
  35.6 1.7 %copy.6 = f32[4,2,4,32,6,128]{5,3,4,2,1,0:T(8,128)} copy(f32[4,2,4,32,6,128]{5,3,4,2,1,0:T(8,128)S(1)} %bitcast.11) | data formatting | bytes 6291456

commit v5 on v4

--- a/solution.py
+++ b/solution.py
@@ -13,7 +13,6 @@
 
 LAYERS, ROWS, LANES = 10, 48, 128
 SEMAPHORES = 56
-OWN_BASE = 2
 OWN_Z = pl.ds(2, 6)
 OWN_X = pl.ds(8, 32)
 RIM_X = {1: pl.ds(6, 2), -1: pl.ds(40, 2)}
@@ -149,7 +148,7 @@
     @pl.when(jnp.logical_or(inner, outer))
     def _():
         greet((fellow, gx, gz))
-        greet((fellow, gx, 3 - gz))
+        greet((lax.rem(h + 4, 8), gx, gz))
 
     @pl.when(has_low)
     def _():
@@ -196,9 +195,18 @@
 
     three = pl.ds(0, 3)
 
-    up = remote(pert.at[pl.ds(4, 4), three], low.at[:, :, OWN_Z, OWN_X], (jnp.minimum(h + 1, 7), gx, gz))
-    down = remote(pert.at[pl.ds(0, 4), three], high.at[:, :, OWN_Z, OWN_X], (jnp.maximum(h - 1, 0), gx, gz))
-    rim_x, base_x, base_mate, base_off, base_own = [], [], [], [], []
+    up, down = [], []
+    for j in range(2):
+        part = pl.ds(2 * j, 2)
+        up.append(remote(pert.at[pl.ds(4 + 2 * j, 2), three], low.at[part, :, OWN_Z, OWN_X], (jnp.minimum(h + 1, 7), gx, gz)))
+        down.append(remote(pert.at[part, three], high.at[part, :, OWN_Z, OWN_X], (jnp.maximum(h - 1, 0), gx, gz)))
+    detour, resume_up, resume_down = [], [], []
+    for z in (0, 3):
+        layers, inside = pl.ds(z, 3), pl.ds(2 + z, 3)
+        detour.append(remote(pert.at[pl.ds(6 - 4 * lax.div(h, 4), 2), three, layers], passing.at[:, :, layers], (fellow, gx, gz)))
+        resume_up.append(onto(up[1], passing.at[:, :, layers], low.at[pl.ds(2, 2), :, inside, OWN_X], (4, gx, gz)))
+        resume_down.append(onto(down[1], passing.at[:, :, layers], high.at[pl.ds(2, 2), :, inside, OWN_X], (3, gx, gz)))
+    rim_x, base_x, base_mate, base_off = [], [], [], []
     for s in (1, -1):
         rim_x.append(remote(pert.at[:, :, :, BARE_X[s]], own.at[:, :, OWN_Z, RIM_X[s]], (h, side_x[s], gz)))
         for ref, at, count in ((mean, 0, 3), (modes, 3, 12)):
@@ -212,14 +220,10 @@
     rim_off = [
         remote(pert.at[half, :, to_off], own.at[half, :, at_off, OWN_X], (h, gx, 3 - gz)) for half in (pl.ds(0, 4), pl.ds(4, 4))
     ]
-    detour = remote(pert.at[pl.ds(4, 4), :, to_off], passing, (fellow, gx, gz))
-    resume = onto(rim_off[1], passing, own.at[pl.ds(4, 4), :, at_off, OWN_X], (fellow, gx, 3 - gz))
     for ref, start, at, count in ((mean, 0, 0, 3), (modes, 0, 3, 6), (modes, 6, 9, 6)):
         source, fields = ref.at[pl.ds(start, count)], pl.ds(at, count)
         base_mate.append(remote(source.at[:, to_mate], flow.at[fields, at_mate, OWN_X], (h, gx, mate)))
         base_off.append(remote(source.at[:, to_off], flow.at[fields, at_off, OWN_X], (lax.rem(h + 4, 8), gx, 3 - gz)))
-        if len(base_own) < OWN_BASE:
-            base_own.append(onto(base_off[-1], source.at[:, to_off], flow.at[fields, at_off, OWN_X], (h, gx, 3 - gz)))
 
     def starts(copies):
         def run():
@@ -242,18 +246,20 @@
 
         return run
 
-    pl.when(has_high)(up.start)
-    pl.when(has_low)(down.start)
-    pl.when(inner)(detour.start)
+    pl.when(inner)(starts(detour))
+    pl.when(has_high)(up[0].start)
+    pl.when(has_low)(down[0].start)
+    cross_up, cross_down = h == 3, h == 4
+    up_here, down_here = has_high & jnp.logical_not(cross_up), has_low & jnp.logical_not(cross_down)
+    pl.when(up_here)(up[1].start)
+    pl.when(down_here)(down[1].start)
     for copy in [*rim_x, *base_x, rim_mate, *base_mate]:
         copy.start()
-
-    @pl.when(jnp.logical_not(inner))
-    def _():
-        starts(rim_off)()
-        starts(base_off)()
-
-    pl.when(inner)(starts(base_off[OWN_BASE:]))
+    normal = jnp.logical_not(jnp.logical_or(inner, outer))
+    pl.when(normal | (h == 7))(rim_off[0].start)
+    pl.when(normal | (h == 0))(rim_off[1].start)
+    for copy in base_off:
+        copy.start()
 
     forward_x, forward_z, straight_z, beside_z, across_z = {}, {}, {}, {}, {}
     for name, ref, side in (("low", low, 1), ("high", high, -1)):
@@ -273,7 +279,6 @@
         beside_z[name] = remote(
             ref.at[:, :, pl.ds(6 - 4 * odd, 2), OWN_X], ref.at[:, :, at_mate, OWN_X], (h, gx, mate)
         )
-    cross_up, cross_down = h == 3, h == 4
     pl.when(cross_up)(straight_z["low"].start)
     pl.when(cross_down)(straight_z["high"].start)
     onward_up, onward_down = has_high & jnp.logical_not(inner), has_low & jnp.logical_not(inner)
@@ -347,11 +352,21 @@
     free, bound = (2 - 2 * odd, 4), (4 * odd, 2)
     mate_edge, off_edge = [far_off, far_off + 1], [off, off + 1]
 
+    def pass_half(i):
+        detour[i].wait_recv()
+        pl.when(h == 0)(resume_up[i].start)
+        pl.when(h == 7)(resume_down[i].start)
+
     sweep([(OWN, (0, 1))], True, chunks=(1, 1, 2))
+
+    @pl.when(outer)
+    def _():
+        pass_half(0)
+
     arrivals(rim_x)()
     pl.when(has_high)(starts(forward_x["low"]))
     pl.when(has_low)(starts(forward_x["high"]))
-    pl.when(inner)(rim_off[0].start)
+    pl.when(inner)(starts(rim_off))
     arrivals(base_x)()
     stage(own, OWN0, middle, x_rims)
     stage(flow_groups, BASE0, middle, x_rims, TWELFTH)
@@ -359,9 +374,9 @@
     def pass_on(j):
         @pl.when(outer & (j == 2))
         def _():
-            detour.wait_recv()
-            resume.start()
-            starts(base_own)()
+            pass_half(1)
+            pl.when(h == 0)(rim_off[0].start)
+            pl.when(h == 7)(rim_off[1].start)
 
     sweep([(OWN, (0, 1))], True, chunks=(0, 3, 2), finish=pass_on)
     arrivals([rim_mate, *base_mate])()
@@ -371,16 +386,17 @@
 
     @pl.when(jnp.logical_not(inner))
     def _():
-        arrivals(rim_off)()
+        pl.when(h != 0)(rim_off[0].wait_recv)
+        pl.when(h != 7)(rim_off[1].wait_recv)
         pl.when(onward_up)(forward_z["low"].start)
         pl.when(onward_down)(forward_z["high"].start)
 
     def neighbours():
-        for present, copy, name, there in ((has_low, up, "low", h == 5), (has_high, down, "high", h == 2)):
+        for present, copies, name, there in ((has_low, up, "low", h == 5), (has_high, down, "high", h == 2)):
 
             @pl.when(present)
-            def _(copy=copy, name=name):
-                copy.wait_recv()
+            def _(copies=copies, name=name):
+                arrivals(copies)()
                 beside_z[name].start()
 
             pl.when(there)(across_z[name].start)
@@ -407,7 +423,8 @@
 
     sweep([(OTHERS, (0, 1, 2))], layers=free)
     sweep([(OTHERS, (0, 1))], layers=bound)
-    pl.when(inner)(arrivals(rim_off))
+    pl.when(inner | (h == 0))(rim_off[0].wait_recv)
+    pl.when(inner | (h == 7))(rim_off[1].wait_recv)
     arrivals(base_off)()
     stage(own, OWN0, off_edge, (OWN_X,))
     stage(flow_groups, BASE0, off_edge, (OWN_X,), TWELFTH)
@@ -419,14 +436,14 @@
             stage(ref, first, off_edge, (OWN_X,))
 
     sweep([(OWN, (2,)), (OTHERS, (2,))], layers=bound)
-    departures([*rim_x, *base_x, rim_mate, rim_off[0], *base_mate])()
-    pl.when(jnp.logical_not(inner))(departures([rim_off[1], *base_off[:OWN_BASE]]))
-    departures(base_off[OWN_BASE:])()
-    pl.when(outer)(departures(base_own))
-    pl.when(inner)(detour.wait_send)
-    pl.when(outer)(resume.wait_send)
-    pl.when(has_high)(up.wait_send)
-    pl.when(has_low)(down.wait_send)
+    departures([*rim_x, *base_x, rim_mate, *rim_off, *base_mate, *base_off])()
+    pl.when(inner)(departures(detour))
+    pl.when(h == 0)(departures(resume_up))
+    pl.when(h == 7)(departures(resume_down))
+    pl.when(has_high)(up[0].wait_send)
+    pl.when(has_low)(down[0].wait_send)
+    pl.when(up_here)(up[1].wait_send)
+    pl.when(down_here)(down[1].wait_send)
     for goes, onward, name in ((has_high, onward_up, "low"), (has_low, onward_down, "high")):
         pl.when(goes)(departures(forward_x[name]))
         pl.when(onward)(forward_z[name].wait_send)
@@ -461,7 +478,7 @@
             pltpu.VMEM((FIELDS, 6, 32, LANES), jnp.float32),
             pltpu.VMEM((32, 6, 32, LANES), jnp.float32),
             pltpu.VMEM((LANES, 2 * LANES), half),
-            pltpu.VMEM((4, 4, 2, 32, LANES), half),
+            pltpu.VMEM((2, 3, 6, 32, LANES), half),
             pltpu.VMEM(mask.shape, jnp.int32),
             pltpu.SemaphoreType.DMA((4,)),
             pltpu.SemaphoreType.DMA((SEMAPHORES,)),

time: 37.3 us -> 32.8 us (0.88)
  the two profiles are of different devices: /device:TPU:68 before, /device:TPU:25 now
where the time goes in v5:
time: 32.8 us; the launch traced here: 32.2 us
  Pallas kernels  30.5 us (93%)
  local copies, waits for them, and re-layouts  1.67 us (5%)
    pallas_call x1, Pallas kernels, shards(): pl.pallas_call(kernel, out_shape=jax.ShapeDtypeStruct(turned.shape, jnp.f...  30.5 us
    unnamed x1, local copies, waits for them, and re-layouts  1.67 us

profile of v5, /device:TPU:25, one launch (start us, length us, event | category | flops | bytes accessed | tf_op | source)
XLA Modules:
  0.0 32.2 jit_solution(3533232102535653230)
XLA Ops:
  0.0 30.5 %shard_map.46 = f32[8,4,6,32,128]{4,3,2,1,0:T(8,128)S(1)} custom-call(bf16[8,4,6,32,128]{4,3,2,1,0:T(8,128)(2,1)} %bitcast.12, bf16[3,6,32,128]{3,2,1,0:T(8,128)(2,1)} %bitcast.14, bf16[12,6,32,128]{3,2,1,0:T(8,128)(2,1)} %bitcast.13, s32[6,32,128]{2,1,0:T(8,128)} %bitcast.15), custom_call_target="tpu_custom_call" | custom-call | tf_op jit(solution)/shard_map/pallas_call | solution.py:467
  30.5 1.7 %copy.6 = f32[4,2,4,32,6,128]{5,3,4,2,1,0:T(8,128)} copy(f32[4,2,4,32,6,128]{5,3,4,2,1,0:T(8,128)S(1)} %bitcast.11) | data formatting | bytes 6291456

commit v6 on v5

--- a/solution.py
+++ b/solution.py
@@ -296,7 +296,7 @@
 
         lax.fori_loop(0, groups, body, 0)
 
-    def stage_own(ref, first, curved, scale=None):
+    def stage_own(ref, first, curved, scale=None, span=None):
         groups, width = ref.shape[:2]
         weights = band[...] if curved else band[:, pl.ds(0, LANES)]
 
@@ -313,7 +313,7 @@
                 bends[fields] = product[:, LANES:].reshape(width, 6, 32, LANES)
             return carry
 
-        lax.fori_loop(0, groups, body, 0)
+        lax.fori_loop(*(span or (0, groups)), body, 0)
 
     middle = range(2, 8)
     flow_groups = flow.reshape(5, 3, LAYERS, ROWS, LANES)
@@ -391,26 +391,36 @@
         pl.when(onward_up)(forward_z["low"].start)
         pl.when(onward_down)(forward_z["high"].start)
 
-    def neighbours():
-        for present, copies, name, there in ((has_low, up, "low", h == 5), (has_high, down, "high", h == 2)):
+    def own_bound():
+        arrivals(base_off)()
+        stage(own, OWN0, off_edge, (OWN_X,))
+        stage(flow_groups, BASE0, off_edge, (OWN_X,), TWELFTH)
+        sweep([(OWN, (2,))], layers=bound)
+
+    pl.when(normal)(own_bound)
+    both = ((has_low, up, low, "low", LOW0, h == 5), (has_high, down, high, "high", HIGH0, h == 2))
+    for j in range(2):
+        for present, copies, ref, name, first, there in both:
 
             @pl.when(present)
-            def _(copies=copies, name=name):
-                arrivals(copies)()
-                beside_z[name].start()
-
-            pl.when(there)(across_z[name].start)
-
-    neighbours()
-    for present, ref, name, first in ((has_low, low, "low", LOW0), (has_high, high, "high", HIGH0)):
+            def _(copies=copies, ref=ref, name=name, first=first):
+                copies[j].wait_recv()
+                if j == 1:
+                    beside_z[name].start()
+
+            if j == 1:
+                pl.when(there)(across_z[name].start)
+
+            @pl.when(present)
+            def _(ref=ref, first=first):
+                stage_own(ref, first, False, span=(2 * j, 2 * j + 2))
+
+    for present, _, ref, name, first, _ in both:
 
         @pl.when(present)
         def _(ref=ref, name=name, first=first):
-            stage_own(ref, first, False)
             arrivals(forward_x[name])()
             stage(ref, first, middle, x_rims)
-            beside_z[name].wait_recv()
-            stage(ref, first, mate_edge, (OWN_X,))
 
         @pl.when(jnp.logical_not(present))
         def _(first=first):
@@ -421,13 +431,18 @@
 
             lax.fori_loop(0, 12, clear, 0)
 
+    sweep([(OTHERS, (0, 1))], layers=bound)
+    for present, _, ref, name, first, _ in both:
+
+        @pl.when(present)
+        def _(ref=ref, name=name, first=first):
+            beside_z[name].wait_recv()
+            stage(ref, first, mate_edge, (OWN_X,))
+
     sweep([(OTHERS, (0, 1, 2))], layers=free)
-    sweep([(OTHERS, (0, 1))], layers=bound)
     pl.when(inner | (h == 0))(rim_off[0].wait_recv)
     pl.when(inner | (h == 7))(rim_off[1].wait_recv)
-    arrivals(base_off)()
-    stage(own, OWN0, off_edge, (OWN_X,))
-    stage(flow_groups, BASE0, off_edge, (OWN_X,), TWELFTH)
+    pl.when(jnp.logical_not(normal))(own_bound)
     for present, ref, name, first in ((has_low, low, "low", LOW0), (has_high, high, "high", HIGH0)):
 
         @pl.when(present)
@@ -435,7 +450,7 @@
             forward_z[name].wait_recv()
             stage(ref, first, off_edge, (OWN_X,))
 
-    sweep([(OWN, (2,)), (OTHERS, (2,))], layers=bound)
+    sweep([(OTHERS, (2,))], layers=bound)
     departures([*rim_x, *base_x, rim_mate, *rim_off, *base_mate, *base_off])()
     pl.when(inner)(departures(detour))
     pl.when(h == 0)(departures(resume_up))

time: 32.8 us -> 31.3 us (0.954); the launches traced: 32.2 us -> 31.1 us
  Pallas kernels: 30.5 us -> 29.5 us
    pallas_call x1, Pallas kernels: 30.5 us -> 29.5 us  [shards(): pl.pallas_call(kernel, out_shape=jax.ShapeDtypeStruct(turned.shape, jnp.f...]
where the time goes in v6:
time: 31.3 us; the launch traced here: 31.1 us
  Pallas kernels  29.5 us (94%)
  local copies, waits for them, and re-layouts  1.67 us (5%)
    pallas_call x1, Pallas kernels, shards(): pl.pallas_call(kernel, out_shape=jax.ShapeDtypeStruct(turned.shape, jnp.f...  29.5 us
    unnamed x1, local copies, waits for them, and re-layouts  1.67 us

profile of v6, /device:TPU:25, one launch (start us, length us, event | category | flops | bytes accessed | tf_op | source)
XLA Modules:
  0.0 31.1 jit_solution(4648895776342921071)
XLA Ops:
  0.0 29.5 %shard_map.46 = f32[8,4,6,32,128]{4,3,2,1,0:T(8,128)S(1)} custom-call(bf16[8,4,6,32,128]{4,3,2,1,0:T(8,128)(2,1)} %bitcast.12, bf16[3,6,32,128]{3,2,1,0:T(8,128)(2,1)} %bitcast.14, bf16[12,6,32,128]{3,2,1,0:T(8,128)(2,1)} %bitcast.13, s32[6,32,128]{2,1,0:T(8,128)} %bitcast.15), custom_call_target="tpu_custom_call" | custom-call | tf_op jit(solution)/shard_map/pallas_call | solution.py:482
  29.5 1.7 %copy.6 = f32[4,2,4,32,6,128]{5,3,4,2,1,0:T(8,128)} copy(f32[4,2,4,32,6,128]{5,3,4,2,1,0:T(8,128)S(1)} %bitcast.11) | data formatting | bytes 6291456
